TPU v7x, 512 devices: a whole 4x8x8 slice. The times are simulated.
512 devices in a mesh: group: 32 (over x, z), local: 16 (over y, core).
Axes of the slice: x: 4, y: 8, z: 8, core: 2. Of those that a mesh axis runs over, the one named last changes fastest.
Arguments:
- tokens: bfloat16 [4096, 3584], P(('group', 'local')), may hold values from -6 to 6
- routes: int32 [4096, 8], P(('group', 'local')), may hold values from 0 to 127, as said below
- route_gates: float32 [4096, 8], P(('group', 'local')), may hold values from 0.2 to 2
- gate_weight: bfloat16 [512, 3584, 256], P(('group', 'local')), may hold values from -0.09375 to 0.09375
- up_weight: bfloat16 [512, 3584, 256], P(('group', 'local')), may hold values from -0.09375 to 0.09375
Outputs:
- routed_hidden: bfloat16 [512, 1024, 256], P(('group', 'local'))
Inputs may be any that keep to these rules, and one draw needn't show every extreme that they name: `routes`: each token names 8 different experts, lying in exactly 4 of the 8 expert groups of 16 consecutive experts; in each aligned block of 4 tokens every block of 4 consecutive experts is used by exactly one token, which names 1 of its experts.
All inputs are finite; a program needn't handle non-finite values.
Results may differ from a plain program's by a relative error of at most 0.012.
Values may be sent and summed in bfloat16 or wider, within the bound.
No kernel may reach another device: no remote copies, remote signals or barrier semaphores. Data moves between devices by JAX's collectives and lax.ppermute only.
A program may use at most 64 MiB of HBM per device.

v0:
```python
import jax
import jax.numpy as jnp
from jax import lax
from jax.sharding import PartitionSpec as P

NEG = 8
EXP_MESH = 4
TOPG = 4
TOP = 8


def over_all(x, axis, dim, block):
    whole = lax.all_gather(x, axis, axis=dim, tiled=True)
    return block(whole, jnp.int32(0))


def pack_rows(tokens, routes, route_gates, n_group):
    quarters = n_group // NEG
    per_token = TOPG * min(TOP // TOPG, quarters)
    per_group = tokens.shape[0] * per_token // n_group
    group_range = jnp.arange(n_group, dtype=jnp.int32)
    member = jnp.any((routes // EXP_MESH)[:, :, None] == group_range[None, None, :], axis=1).astype(
        jnp.int32
    )
    position = jnp.cumsum(member, axis=0) - 1
    slot_range = jnp.arange(per_group, dtype=jnp.int32)
    chosen = (member.T[:, None, :] == 1) & (position.T[:, None, :] == slot_range[None, :, None])
    packed = jnp.einsum(
        "gjt,td->gjd", chosen.astype(jnp.bfloat16), tokens, preferred_element_type=jnp.float32
    ).astype(jnp.bfloat16)
    expert_grid = group_range[:, None] * EXP_MESH + jnp.arange(EXP_MESH, dtype=jnp.int32)[None, :]
    matches = (routes[:, :, None, None] == expert_grid[None, None, :, :]).astype(jnp.float32)
    dense_gates = jnp.sum(route_gates[:, :, None, None] * matches, axis=1)
    packed_gates = jnp.einsum(
        "gjt,tgs->gjs", chosen.astype(jnp.float32), dense_gates, precision=lax.Precision.HIGHEST
    )
    return (packed, packed_gates)


def expand(token_rows, row_gates, gate_weight, up_weight, slot_index):
    lead_shape = token_rows.shape[:-1]
    flat_rows = token_rows.reshape(-1, token_rows.shape[-1])
    picker = (jnp.arange(row_gates.shape[-1], dtype=jnp.int32) == slot_index).astype(jnp.float32)
    scaling = jnp.sum(row_gates * picker, axis=-1).reshape(-1, 1)
    pre_gate = jnp.dot(flat_rows, gate_weight[0], preferred_element_type=jnp.float32)
    pre_up = jnp.dot(flat_rows, up_weight[0], preferred_element_type=jnp.float32)
    hidden = (jax.nn.silu(pre_gate) * pre_up * scaling).astype(jnp.bfloat16)
    return hidden.reshape(lead_shape + (hidden.shape[-1],))


def shards(tokens, routes, route_gates, gate_weight, up_weight):
    n_group = lax.axis_size("group")
    slot_index = lax.axis_index("local") // (lax.axis_size("local") // EXP_MESH)
    packed, packed_gates = pack_rows(tokens, routes, route_gates, n_group)

    def compute_pieces(pieces_in):
        return expand(pieces_in[0], pieces_in[1], gate_weight, up_weight, slot_index)

    received = (
        lax.all_to_all(packed, "group", split_axis=0, concat_axis=0, tiled=True),
        lax.all_to_all(
            packed_gates.astype(jnp.bfloat16), "group", split_axis=0, concat_axis=0, tiled=True
        ).astype(packed_gates.dtype),
    )
    result = over_all(
        (received[0], received[1].astype(jnp.bfloat16)),
        "local",
        1,
        lambda piece, start: compute_pieces((piece[0], piece[1].astype(jnp.float32))),
    )
    return result.reshape(1, -1, result.shape[-1])


def solution(mesh):
    placed = (
        P(("group", "local"), None),
        P(("group", "local"), None),
        P(("group", "local"), None),
        P(("group", "local"), None, None),
        P(("group", "local"), None, None),
    )
    return jax.shard_map(
        shards,
        mesh=mesh,
        in_specs=placed,
        out_specs=P(("group", "local"), None, None),
        check_vma=False,
    )
```

profile of v0, /device:TPU:1, one launch (start us, length us, event | category | flops | bytes accessed | tf_op | source)
XLA Modules:
  0.0 109.3 jit_solution(4208281942131699710)
XLA Ops:
  6.5 0.8 add_select_fusion
  7.4 0.1 fusion.17
  7.5 0.1 copy.25
  7.6 0.1 copy.26
  7.7 1.1 convolution_convert_fusion
  8.8 0.5 copy.28
  9.3 26.5 %all_to_all.10 = bf16[32,2,3584]{2,1,0:T(2,128)(2,1)S(1)} all-to-all(bf16[32,2,3584]{2,1,0:T(2,128)(2,1)S(1)} %copy.28), channel_id=1, replica_groups=mesh['group'=32,'local'=16] {'group'}, dimensions={0} | all-to-all | bytes 917504 | tf_op jit(solution)/shard_map/all_to_all | solution.py:60
  35.8 0.8 copy.29
  36.6 0.0 all-gather.2.cloned.1.call-update
  36.6 0.8 select_reduce_fusion
  37.5 0.1 copy.31
  37.6 0.9 convolution_convert_fusion.1
  38.4 7.7 %all-to-all-start.1 = ((bf16[32,2,4]{2,1,0:T(2,128)(2,1)}), bf16[32,2,4]{2,1,0:T(2,128)(2,1)S(1)}, u32[]{:S(2)}, u32[]{:S(2)}) async-start(bf16[32,2,4]{2,1,0:T(2,128)(2,1)} %convolution_convert_fusion.1), calls=%async_computation.1 | async-start | bytes 32768 | tf_op jit(solution)/shard_map/all_to_all | solution.py:61
  46.2 8.6 %all-to-all-done.1 = bf16[32,2,4]{2,1,0:T(2,128)(2,1)S(1)} async-done(((bf16[32,2,4]{2,1,0:T(2,128)(2,1)}), bf16[32,2,4]{2,1,0:T(2,128)(2,1)S(1)}, u32[]{:S(2)}, u32[]{:S(2)}) %all-to-all-start.1) | async-done | bytes 544 | tf_op jit(solution)/shard_map/all_to_all | solution.py:61
  54.8 0.1 copy.32
  54.9 20.6 %all_gather.7 = bf16[32,32,4]{0,2,1:T(4,128)(2,1)S(1)} all-gather(bf16[32,2,4]{0,2,1:T(4,128)(2,1)S(1)} %copy.32), channel_id=1, replica_groups=mesh['group'=32,'local'=16] {'local'}, dimensions={1}, use_global_device_ids=true | all-gather | bytes 8704 | tf_op jit(solution)/shard_map/all_gather | solution.py:13
  75.5 0.1 multiply_reduce_fusion
  75.6 0.1 copy.33
  75.7 0.1 mul.52
  75.8 14.6 %all-gather.2.cloned.1.call-done = bf16[32,32,3584]{2,0,1:T(8,128)(2,1)} async-done(((bf16[32,2,3584]{2,0,1:T(8,128)(2,1)}), bf16[32,32,3584]{2,0,1:T(8,128)(2,1)}) %all-gather.2.cloned.1.call-update) | async-done | bytes 7340048 | tf_op jit(solution)/shard_map/all_gather | solution.py:13
  90.4 7.1 %copy.30 = bf16[32,32,3584]{2,1,0:T(8,128)(2,1)S(1)} copy(bf16[32,32,3584]{2,0,1:T(8,128)(2,1)} %all-gather.2.cloned.1.call-done) | data formatting | bytes 14680064 | tf_op jit(solution)/shard_map/all_gather | solution.py:13
  97.5 0.0 copy-start.1
  97.5 2.1 %fusion.2 = f32[1024,256]{1,0:T(8,128)S(1)} fusion(bf16[1024,3584]{1,0:T(8,128)(2,1)S(1)} %bitcast.28, bf16[1,3584,256]{2,1,0:T(8,128)(2,1)S(1)} %copy-done), kind=kOutput, calls=%fused_computation.3 | convolution fusion | flops 1879048192 | bytes 10223616 | tf_op jit(solution)/shard_map/dot_general | solution.py:45
  99.6 2.9 %fusion.13 = bf16[1,1024,256]{2,1,0:T(8,128)(2,1)} fusion(bf16[1024,3584]{1,0:T(8,128)(2,1)S(1)} %bitcast.29, bf16[1,3584,256]{2,1,0:T(8,128)(2,1)S(1)} %copy-done.1, f32[1024,256]{1,0:T(8,128)S(1)} %fusion.2, f32[1024]{0:T(1024)S(1)} %mul.52), kind=kOutput, calls=%fused_computation.8 | convolution fusion | flops 1880883200 | bytes 10752000 | tf_op jit(solution)/shard_map/dot_general | solution.py:46
  (11 shorter events, 0.1 us)
Async XLA Ops:
  6.5 91.0 %copy-start = (bf16[1,3584,256]{2,1,0:T(8,128)(2,1)S(1)}, bf16[1,3584,256]{2,1,0:T(8,128)(2,1)}, u32[]{:S(2)}) copy-start(bf16[1,3584,256]{2,1,0:T(8,128)(2,1)} %param.8) | copy-start | bytes 5505028
  6.5 83.9 %all-gather.2.cloned.1.call-start = ((), (), s32[]{:S(2)}) async-start(), calls=%async_computation.2 | async-start | bytes 7798784 | tf_op jit(solution)/shard_map/all_gather | solution.py:13
  38.4 16.3 %all-to-all-start.1 = ((bf16[32,2,4]{2,1,0:T(2,128)(2,1)}), bf16[32,2,4]{2,1,0:T(2,128)(2,1)S(1)}, u32[]{:S(2)}, u32[]{:S(2)}) async-start(bf16[32,2,4]{2,1,0:T(2,128)(2,1)} %convolution_convert_fusion.1), calls=%async_computation.1 | async-start | bytes 32768 | tf_op jit(solution)/shard_map/all_to_all | solution.py:61
  97.5 2.1 %copy-start.1 = (bf16[1,3584,256]{2,1,0:T(8,128)(2,1)S(1)}, bf16[1,3584,256]{2,1,0:T(8,128)(2,1)}, u32[]{:S(2)}) copy-start(bf16[1,3584,256]{2,1,0:T(8,128)(2,1)} %param.9) | copy-start | bytes 5505028
Sparse Core Ops, SparseCore 0:
  36.7 53.6 all-gather.1
where the time goes:
time: 110 us; the launch traced here: 109 us
  blocking collectives  47.1 us (43%)
  waiting for transfers between devices  23.3 us (21%)
  between operations  13.5 us (12%)
  local copies, waits for them, and re-layouts  8.9 us (8%)
  starting transfers between devices  7.69 us (7%)
  matrix products  6.87 us (6%)
  other arithmetic  1.95 us (2%)
    all_to_all x1, blocking collectives, shards(): lax.all_to_all(packed, 'group', split_axis=0, concat_axis=0, tiled=True)  26.5 us
    all_gather x1, blocking collectives, over_all(): whole = lax.all_gather(x, axis, axis=dim, tiled=True)  20.6 us
    all_gather x1, waiting for transfers between devices, over_all(): whole = lax.all_gather(x, axis, axis=dim, tiled=True)  14.6 us
    all_to_all x1, waiting for transfers between devices, shards(): lax.all_to_all(packed_gates.astype(jnp.bfloat16), 'group', split_axis=0,...  8.62 us
    all_to_all x1, starting transfers between devices, shards(): lax.all_to_all(packed_gates.astype(jnp.bfloat16), 'group', split_axis=0,...  7.69 us
    all_gather x1, local copies, waits for them, and re-layouts, over_all(): whole = lax.all_gather(x, axis, axis=dim, tiled=True)  7.1 us
    dot_general x1, matrix products, expand(): jnp.dot(flat_rows, up_weight[0], preferred_element_type=jnp.float32)  2.88 us
  transfers between devices with their start and end apart: 2, of which 2 were waited for; matrix products, arithmetic and copies ran while one was open for 2% of the time, Pallas kernels for 0%

commit v1 on v0

v1 whole, which is shorter than its diff:
```python
import jax
import jax.numpy as jnp
from jax import lax
from jax.experimental import pallas as pl
from jax.experimental.pallas import tpu as pltpu
from jax.sharding import PartitionSpec as P

EXP_MESH = 4
BLOCK = 4
GATE_ONE = 16000.0
CODE_MAX = 32000.0
EXP_BIAS = 200.0


def pack_kernel(tokens_ref, routes_ref, gates_ref, out_ref):
    count, width = tokens_ref.shape
    rows = out_ref.shape[0]
    per_group = count // BLOCK
    experts = out_ref.shape[1] - width
    tok = tokens_ref[...].astype(jnp.float32)
    largest = jnp.maximum(jnp.max(jnp.abs(tok), axis=1, keepdims=True), 1e-25)
    power = jnp.floor(jnp.log2(CODE_MAX / largest))
    codes = jnp.round(tok * jnp.exp2(power))
    routes = routes_ref[...]
    gate_codes = jnp.round(gates_ref[...] * GATE_ONE)
    expert = lax.broadcasted_iota(jnp.int32, (count, experts), 1)
    row = lax.broadcasted_iota(jnp.int32, (count, rows), 1)
    token = lax.broadcasted_iota(jnp.int32, (count, rows), 0)
    side = jnp.zeros((count, experts), jnp.float32)
    chosen = jnp.zeros((count, rows), jnp.float32)
    for k in range(routes.shape[1]):
        route = routes[:, k : k + 1]
        side = side + jnp.where(expert == route, gate_codes[:, k : k + 1], 0.0)
        chosen = jnp.where(route // EXP_MESH == row // per_group, 1.0, chosen)
    side = jnp.where(side > 0.0, side, -(power + EXP_BIAS))
    chosen = jnp.where(token // BLOCK == row % per_group, chosen, 0.0)
    chosen = chosen.T.astype(jnp.bfloat16)

    def send(values, first, size):
        high = jnp.floor(values * (1.0 / 256.0))
        low = values - 256.0 * high
        picked = jnp.dot(chosen, (256.0 * high).astype(jnp.bfloat16), preferred_element_type=jnp.float32)
        picked += jnp.dot(chosen, low.astype(jnp.bfloat16), preferred_element_type=jnp.float32)
        out_ref[:, first : first + size] = picked.astype(jnp.int32).astype(jnp.int16)

    send(codes, 0, width)
    send(side, width, experts)


def pack_rows(tokens, routes, route_gates, n_group, experts):
    count, width = tokens.shape
    rows = n_group * (count // BLOCK)
    return pl.pallas_call(
        pack_kernel,
        out_shape=jax.ShapeDtypeStruct((rows, width + experts), jnp.int16),
        in_specs=[pl.BlockSpec(memory_space=pltpu.VMEM)] * 3,
        out_specs=pl.BlockSpec(memory_space=pltpu.VMEM),
    )(tokens, routes, route_gates)


def shards(tokens, routes, route_gates, gate_weight, up_weight):
    n_group = lax.axis_size("group")
    n_local = lax.axis_size("local")
    n_y = n_local // 2
    width = tokens.shape[1]
    experts = n_group * EXP_MESH
    per_group = tokens.shape[0] // BLOCK
    local = lax.axis_index("local")
    core = local % 2
    my_expert = lax.axis_index("group") * EXP_MESH + local // (n_local // EXP_MESH)
    swap = [(2 * y + c, 2 * y + 1 - c) for y in range(n_y) for c in range(2)]
    same_core = [[2 * y + c for y in range(n_y)] for c in range(2)]

    other_gate = lax.ppermute(gate_weight, "local", swap)
    other_up = lax.ppermute(up_weight, "local", swap)

    packed = pack_rows(tokens, routes, route_gates, n_group, experts)
    packed = packed.reshape(n_group, per_group, width + experts)
    received = lax.all_to_all(packed, "group", split_axis=0, concat_axis=0, tiled=True)
    received = received.reshape(1, n_group * per_group, width + experts)
    gathered = lax.all_gather(received, "local", axis=0, axis_index_groups=same_core, tiled=True)
    gathered = gathered.reshape(-1, width + experts)

    rows = gathered[:, :width].astype(jnp.bfloat16)
    side = gathered[:, width:].astype(jnp.float32)
    scale = jnp.exp2(jnp.min(side, axis=1, keepdims=True) + EXP_BIAS)
    mine = lax.broadcasted_iota(jnp.int32, (1, experts), 1) == my_expert
    weight = jnp.sum(jnp.where(mine, jnp.maximum(side, 0.0), 0.0), axis=1, keepdims=True)
    weight = weight * (1.0 / GATE_ONE)

    def hidden(gate, up):
        pre_gate = jnp.dot(rows, gate[0], preferred_element_type=jnp.float32) * scale
        pre_up = jnp.dot(rows, up[0], preferred_element_type=jnp.float32) * scale
        return (jax.nn.silu(pre_gate) * pre_up * weight).astype(jnp.bfloat16)

    for_other = hidden(other_gate, other_up)
    from_other = lax.ppermute(for_other, "local", swap)
    own = hidden(gate_weight, up_weight)
    out_dim = own.shape[-1]

    first = jnp.where(core == 0, own, from_other).reshape(n_y, n_group, 1, per_group, out_dim)
    second = jnp.where(core == 0, from_other, own).reshape(n_y, n_group, 1, per_group, out_dim)
    both = jnp.concatenate([first, second], axis=2)
    return jnp.transpose(both, (1, 0, 2, 3, 4)).reshape(1, -1, out_dim)


def solution(mesh):
    placed = (
        P(("group", "local"), None),
        P(("group", "local"), None),
        P(("group", "local"), None),
        P(("group", "local"), None, None),
        P(("group", "local"), None, None),
    )
    return jax.shard_map(
        shards,
        mesh=mesh,
        in_specs=placed,
        out_specs=P(("group", "local"), None, None),
        check_vma=False,
    )
```

time: 110 us -> 89.1 us (0.81)
  starting transfers between devices: 7.69 us -> 24.9 us
  waiting for transfers between devices: 23.3 us -> 8.4 us
  between operations: 13.5 us -> 0.19 us
  blocking collectives: 47.1 us -> 39.3 us
  local copies, waits for them, and re-layouts: 8.9 us -> 4.09 us
  Pallas kernels: 0 us -> 2.18 us
  matrix products: 6.87 us -> 8.28 us
    all_to_all x1 -> x0, blocking collectives: 26.5 us -> none  [shards(): lax.all_to_all(packed, 'group', split_axis=0, concat_axis=0, tiled=True)]
    all_gather x1, blocking collectives: 20.6 us -> 39.3 us  [shards(): lax.all_gather(received, 'local', axis=0, axis_index_groups=same_core, ti...]
    all_gather x1 -> x0, waiting for transfers between devices: 14.6 us -> none  [over_all(): whole = lax.all_gather(x, axis, axis=dim, tiled=True)]
    ppermute x0 -> x3, starting transfers between devices: none -> 11.2 us  [the longest x1 6.4 us: shards(): from_other = lax.ppermute(for_other, 'local', swap)]
    all_gather x1 -> x0, local copies, waits for them, and re-layouts: 7.1 us -> none  [over_all(): whole = lax.all_gather(x, axis, axis=dim, tiled=True)]
    all_to_all x1, starting transfers between devices: 7.69 us -> 13.7 us  [shards(): lax.all_to_all(packed, 'group', split_axis=0, concat_axis=0, tiled=True)]
    reshape x0 -> x5, local copies, waits for them, and re-layouts: none -> 3.54 us  [the longest x1 2.14 us: shards(): packed = packed.reshape(n_group, per_group, width + experts)]
    pallas_call x0 -> x1, Pallas kernels: none -> 2.18 us  [pack_rows(): pl.pallas_call(pack_kernel, out_shape=jax.ShapeDtypeStruct((rows, width +...]
  transfers between devices with their start and end apart: 2 -> 4, of which waited for: 2 -> 1; matrix products, arithmetic and copies ran while one was open for 2% -> 7% of each run, Pallas kernels for 0% -> 0%
where the time goes in v1:
time: 89.1 us; the launch traced here: 88.3 us
  blocking collectives  39.3 us (44%)
  starting transfers between devices  24.9 us (28%)
  waiting for transfers between devices  8.4 us (9%)
  matrix products  8.28 us (9%)
  local copies, waits for them, and re-layouts  4.09 us (5%)
  Pallas kernels  2.18 us (2%)
  other arithmetic  1.01 us (1%)
    all_gather x1, blocking collectives, shards(): lax.all_gather(received, 'local', axis=0, axis_index_groups=same_core, ti...  39.3 us
    all_to_all x1, starting transfers between devices, shards(): lax.all_to_all(packed, 'group', split_axis=0, concat_axis=0, tiled=True)  13.7 us
    all_to_all x1, waiting for transfers between devices, shards(): lax.all_to_all(packed, 'group', split_axis=0, concat_axis=0, tiled=True)  8.39 us
    ppermute x1, starting transfers between devices, shards(): from_other = lax.ppermute(for_other, 'local', swap)  6.4 us
    dot_general x2, matrix products, hidden(): pre_up = jnp.dot(rows, up[0], preferred_element_type=jnp.float32) * scale  4.27 us
    dot_general x2, matrix products, hidden(): jnp.dot(rows, gate[0], preferred_element_type=jnp.float32) * scale  4.01 us
    ppermute x1, starting transfers between devices, shards(): other_gate = lax.ppermute(gate_weight, 'local', swap)  2.87 us
    pallas_call x1, Pallas kernels, pack_rows(): pl.pallas_call(pack_kernel, out_shape=jax.ShapeDtypeStruct((rows, width +...  2.18 us
  transfers between devices with their start and end apart: 4, of which 1 were waited for; matrix products, arithmetic and copies ran while one was open for 7% of the time, Pallas kernels for 0%

profile of v1, /device:TPU:1, one launch (start us, length us, event | category | flops | bytes accessed | tf_op | source)
XLA Modules:
  0.0 88.3 jit_solution(2788500965450444335)
XLA Ops:
  0.0 2.2 %shard_map.55 = s16[64,3712]{1,0:T(8,128)(2,1)} custom-call(bf16[8,3584]{1,0:T(8,128)(2,1)} %tokens_ref.1, s32[8,8]{1,0:T(8,128)} %routes_ref.1, f32[8,8]{1,0:T(8,128)} %gates_ref.1), custom_call_target="tpu_custom_call" | custom-call | tf_op jit(solution)/shard_map/pallas_call | solution.py:53
  2.2 2.1 %reshape.35 = s16[32,2,3712]{2,1,0:T(2,128)(2,1)} reshape(s16[64,3712]{1,0:T(8,128)(2,1)} %shard_map.55) | data formatting | bytes 950272 | tf_op jit(solution)/shard_map/reshape | solution.py:78
  4.3 13.7 %all-to-all-start = ((s16[32,2,3712]{2,1,0:T(2,128)(2,1)}), s16[32,2,3712]{2,1,0:T(2,128)(2,1)S(1)}, u32[]{:S(2)}, u32[]{:S(2)}) async-start(s16[32,2,3712]{2,1,0:T(2,128)(2,1)} %reshape.35), calls=%async_computation | async-start | bytes 950272 | tf_op jit(solution)/shard_map/all_to_all | solution.py:79
  18.0 2.9 %collective-permute-start = (bf16[1,3584,256]{2,1,0:T(8,128)(2,1)}, bf16[1,3584,256]{2,1,0:T(8,128)(2,1)}, u32[]{:S(2)}, u32[]{:S(2)}) collective-permute-start(bf16[1,3584,256]{2,1,0:T(8,128)(2,1)} %param.8), channel_id=1, source_target_pairs={{0,1},{1,0},{2,3},{3,2},{4,5},{5,4},{6,7},{7,6},{8,9},{9,8},{10,11... | collective-permute-start | bytes 5505032 | tf_op jit(solution)/shard_map/ppermute | solution.py:74
  20.9 1.9 %collective-permute-start.1 = (bf16[1,3584,256]{2,1,0:T(8,128)(2,1)}, bf16[1,3584,256]{2,1,0:T(8,128)(2,1)}, u32[]{:S(2)}, u32[]{:S(2)}) collective-permute-start(bf16[1,3584,256]{2,1,0:T(8,128)(2,1)} %param.9), channel_id=1, source_target_pairs={{0,1},{1,0},{2,3},{3,2},{4,5},{5,4},{6,7},{7,6},{8,9},{9,8},{10,11... | collective-permute-start | bytes 5505032 | tf_op jit(solution)/shard_map/ppermute | solution.py:75
  22.9 8.4 %all-to-all-done = s16[32,2,3712]{2,1,0:T(2,128)(2,1)S(1)} async-done(((s16[32,2,3712]{2,1,0:T(2,128)(2,1)}), s16[32,2,3712]{2,1,0:T(2,128)(2,1)S(1)}, u32[]{:S(2)}, u32[]{:S(2)}) %all-to-all-start) | async-done | bytes 475168 | tf_op jit(solution)/shard_map/all_to_all | solution.py:79
  31.3 0.2 reshape.36
  31.5 39.3 %all-gather.1 = s16[8,64,3712]{2,1,0:T(8,128)(2,1)S(1)} all-gather(s16[1,64,3712]{2,1,0:T(8,128)(2,1)S(1)} %reshape.36), channel_id=1, replica_groups={{0,2,4,6,8,10,12,14},{1,3,5,7,9,11,13,15},{16,18,20,22,24,26,28,30},{17..., dimensions={0}, use_global_device_ids=true | all-gather | bytes 4276224 | tf_op jit(solution)/shard_map/all_gather | solution.py:81
  70.8 0.2 fusion.30
  71.0 0.0 copy-done
  71.0 1.3 %fusion.8 = f32[512,256]{1,0:T(8,128)S(1)} fusion(bf16[1,3584,256]{2,1,0:T(8,128)(2,1)S(1)} %copy-done, s16[512,3712]{1,0:T(8,128)(2,1)S(1)} %bitcast.32, f32[512]{0:T(512)S(1)} %get-tuple-element.9), kind=kOutput, calls=%fused_computation.9 | convolution fusion | flops 941490176 | bytes 6031360 | tf_op jit(solution)/shard_map/dot_general | solution.py:92
  72.3 0.0 collective-permute-done
  72.3 2.8 %fusion.17 = f32[512,256]{1,0:T(8,128)S(1)} fusion(bf16[1,3584,256]{2,1,0:T(8,128)(2,1)} %collective-permute-done, s16[512,3712]{1,0:T(8,128)(2,1)S(1)} %bitcast.33, f32[512]{0:T(512)S(1)} %get-tuple-element.9), kind=kOutput, calls=%fused_computation.12 | convolution fusion | flops 941490176 | bytes 6031360 | tf_op jit(solution)/shard_map/dot_general | solution.py:92
  75.1 0.0 collective-permute-done.1
  75.1 0.0 copy-start.1
  75.1 3.0 %multiply_convert_fusion = bf16[512,256]{1,0:T(8,128)(2,1)S(1)} fusion(f32[512,256]{1,0:T(8,128)S(1)} %fusion.17, f32[512]{0:T(512)S(1)} %get-tuple-element.10, f32[512]{0:T(512)S(1)} %get-tuple-element.9, bf16[1,3584,256]{2,1,0:T(8,128)(2,1)} %collective-permute-done.1, s16[512,3712]{1,0:T(8,128)(2,1)S(1)} %bitcast.34), kind=kOutput, calls=%fused_computation.17 | convolution fusion | flops 942407680 | bytes 6295552 | tf_op jit(solution)/shard_map/dot_general | solution.py:93
  78.0 6.4 %collective-permute-start.2 = (bf16[512,256]{1,0:T(8,128)(2,1)S(1)}, bf16[512,256]{1,0:T(8,128)(2,1)S(1)}, u32[]{:S(2)}, u32[]{:S(2)}) collective-permute-start(bf16[512,256]{1,0:T(8,128)(2,1)S(1)} %multiply_convert_fusion), channel_id=1, source_target_pairs={{0,1},{1,0},{2,3},{3,2},{4,5},{5,4},{6,7},{7,6},{8,9},{9,8},{10,11... | collective-permute-start | bytes 786440 | tf_op jit(solution)/shard_map/ppermute | solution.py:97
  84.4 1.3 %fusion.26 = bf16[512,256]{1,0:T(8,128)(2,1)S(1)} fusion(bf16[1,3584,256]{2,1,0:T(8,128)(2,1)S(1)} %copy-done.1, s16[512,3712]{1,0:T(8,128)(2,1)S(1)} %bitcast.35, f32[512,256]{1,0:T(8,128)S(1)} %fusion.8, f32[512]{0:T(512)S(1)} %get-tuple-element.10, f32[512]{0:T(512)S(1)} %get-tuple-element.9), kind=kOutput, calls=%fused_computation.15 | convolution fusion | flops 942407680 | bytes 6295552 | tf_op jit(solution)/shard_map/dot_general | solution.py:93
  85.8 0.0 collective-permute-done.2
  85.8 0.1 reshape.38
  85.9 0.1 reshape.39
  86.1 0.7 maximum_bitcast_fusion
  86.8 0.5 copy.7
  87.3 1.0 %reshape.40 = bf16[1,1024,256]{2,1,0:T(8,128)(2,1)} reshape(bf16[32,8,2,2,256]{4,3,2,1,0:T(2,128)(2,1)S(1)} %copy.7) | data formatting | bytes 1048576 | tf_op jit(solution)/shard_map/reshape | solution.py:104
  (5 shorter events, 0.1 us)
Async XLA Ops:
  2.2 68.8 %copy-start = (bf16[1,3584,256]{2,1,0:T(8,128)(2,1)S(1)}, bf16[1,3584,256]{2,1,0:T(8,128)(2,1)}, u32[]{:S(2)}) copy-start(bf16[1,3584,256]{2,1,0:T(8,128)(2,1)} %param.8) | copy-start | bytes 5505028
  4.3 26.9 %all-to-all-start = ((s16[32,2,3712]{2,1,0:T(2,128)(2,1)}), s16[32,2,3712]{2,1,0:T(2,128)(2,1)S(1)}, u32[]{:S(2)}, u32[]{:S(2)}) async-start(s16[32,2,3712]{2,1,0:T(2,128)(2,1)} %reshape.35), calls=%async_computation | async-start | bytes 950272 | tf_op jit(solution)/shard_map/all_to_all | solution.py:79
  18.0 54.3 %collective-permute-start = (bf16[1,3584,256]{2,1,0:T(8,128)(2,1)}, bf16[1,3584,256]{2,1,0:T(8,128)(2,1)}, u32[]{:S(2)}, u32[]{:S(2)}) collective-permute-start(bf16[1,3584,256]{2,1,0:T(8,128)(2,1)} %param.8), channel_id=1, source_target_pairs={{0,1},{1,0},{2,3},{3,2},{4,5},{5,4},{6,7},{7,6},{8,9},{9,8},{10,11... | collective-permute-start | bytes 5505032 | tf_op jit(solution)/shard_map/ppermute | solution.py:74
  20.9 54.1 %collective-permute-start.1 = (bf16[1,3584,256]{2,1,0:T(8,128)(2,1)}, bf16[1,3584,256]{2,1,0:T(8,128)(2,1)}, u32[]{:S(2)}, u32[]{:S(2)}) collective-permute-start(bf16[1,3584,256]{2,1,0:T(8,128)(2,1)} %param.9), channel_id=1, source_target_pairs={{0,1},{1,0},{2,3},{3,2},{4,5},{5,4},{6,7},{7,6},{8,9},{9,8},{10,11... | collective-permute-start | bytes 5505032 | tf_op jit(solution)/shard_map/ppermute | solution.py:75
  75.1 9.4 %copy-start.1 = (bf16[1,3584,256]{2,1,0:T(8,128)(2,1)S(1)}, bf16[1,3584,256]{2,1,0:T(8,128)(2,1)}, u32[]{:S(2)}) copy-start(bf16[1,3584,256]{2,1,0:T(8,128)(2,1)} %param.9) | copy-start | bytes 5505028
  78.0 7.7 %collective-permute-start.2 = (bf16[512,256]{1,0:T(8,128)(2,1)S(1)}, bf16[512,256]{1,0:T(8,128)(2,1)S(1)}, u32[]{:S(2)}, u32[]{:S(2)}) collective-permute-start(bf16[512,256]{1,0:T(8,128)(2,1)S(1)} %multiply_convert_fusion), channel_id=1, source_target_pairs={{0,1},{1,0},{2,3},{3,2},{4,5},{5,4},{6,7},{7,6},{8,9},{9,8},{10,11... | collective-permute-start | bytes 786440 | tf_op jit(solution)/shard_map/ppermute | solution.py:97

commit v2 on v1

v2 whole, which is shorter than its diff:
```python
import functools

import jax
import jax.numpy as jnp
from jax import lax
from jax.experimental import pallas as pl
from jax.experimental.pallas import tpu as pltpu
from jax.sharding import PartitionSpec as P

EXP_MESH = 4
BLOCK = 4
LANES = 128
GATE_ONE = 16000.0
CODE_MAX = 32000.0
EXP_BIAS = 200.0


def pack_kernel(tokens_ref, routes_ref, gates_ref, out_ref):
    count, width = tokens_ref.shape
    n_group, per_group, packed_width = out_ref.shape
    rows = n_group * per_group
    experts = packed_width - width
    tok = tokens_ref[...].astype(jnp.float32)
    largest = jnp.maximum(jnp.max(jnp.abs(tok), axis=1, keepdims=True), 1e-25)
    power = jnp.floor(jnp.log2(CODE_MAX / largest))
    codes = jnp.round(tok * jnp.exp2(power))
    routes = routes_ref[...]
    gate_codes = jnp.round(gates_ref[...] * GATE_ONE)
    expert = lax.broadcasted_iota(jnp.int32, (count, experts), 1)
    row = lax.broadcasted_iota(jnp.int32, (count, rows), 1)
    token = lax.broadcasted_iota(jnp.int32, (count, rows), 0)
    side = jnp.zeros((count, experts), jnp.float32)
    chosen = jnp.zeros((count, rows), jnp.float32)
    for k in range(routes.shape[1]):
        route = routes[:, k : k + 1]
        side = side + jnp.where(expert == route, gate_codes[:, k : k + 1], 0.0)
        chosen = jnp.where(route // EXP_MESH == row // per_group, 1.0, chosen)
    side = jnp.where(side > 0.0, side, -(power + EXP_BIAS))
    chosen = jnp.where(token // BLOCK == row % per_group, chosen, 0.0)
    chosen = chosen.T.astype(jnp.bfloat16)

    def send(values, first, size):
        high = jnp.floor(values * (1.0 / 256.0))
        low = values - 256.0 * high
        picked = jnp.dot(chosen, (256.0 * high).astype(jnp.bfloat16), preferred_element_type=jnp.float32)
        picked += jnp.dot(chosen, low.astype(jnp.bfloat16), preferred_element_type=jnp.float32)
        picked = picked.astype(jnp.int32).astype(jnp.int16)
        for group in range(n_group):
            out_ref[group, :, first : first + size] = picked[group * per_group : (group + 1) * per_group]

    send(codes, 0, width)
    send(side, width, experts)


def pack_rows(tokens, routes, route_gates, n_group, experts):
    count, width = tokens.shape
    return pl.pallas_call(
        pack_kernel,
        out_shape=jax.ShapeDtypeStruct((n_group, count // BLOCK, width + experts), jnp.int16),
        in_specs=[pl.BlockSpec(memory_space=pltpu.VMEM)] * 3,
        out_specs=pl.BlockSpec(memory_space=pltpu.VMEM),
    )(tokens, routes, route_gates)


def hidden_kernel(expert_ref, codes_ref, *refs):
    weights, (other_ref, own_ref), (rows, held, arrived) = refs[:4], refs[4:6], refs[6:]
    width = rows.shape[1]
    copies = [pltpu.make_async_copy(weights[j], held.at[j], arrived.at[j]) for j in range(4)]
    for copy in copies:
        copy.start()
    rows[...] = codes_ref[:, :width].astype(jnp.float32).astype(jnp.bfloat16)
    side = codes_ref[:, width:].astype(jnp.float32)
    lane = lax.broadcasted_iota(jnp.int32, side.shape, 1)
    weight = jnp.sum(jnp.where(lane == expert_ref[0], jnp.maximum(side, 0.0), 0.0), axis=1, keepdims=True)
    weight = weight * (1.0 / GATE_ONE)
    scale = jnp.exp2(jnp.min(side, axis=1, keepdims=True) + EXP_BIAS)
    for first, out_ref in ((0, other_ref), (2, own_ref)):
        copies[first].wait()
        pre_gate = jnp.dot(rows[...], held[first], preferred_element_type=jnp.float32) * scale
        copies[first + 1].wait()
        pre_up = jnp.dot(rows[...], held[first + 1], preferred_element_type=jnp.float32) * scale
        out_ref[...] = (pre_gate / (1.0 + jnp.exp(-pre_gate)) * pre_up * weight).astype(out_ref.dtype)


def multiply(expert, codes, width, weights):
    count = codes.shape[0]
    depth, out_dim = weights[0].shape
    return pl.pallas_call(
        hidden_kernel,
        out_shape=[jax.ShapeDtypeStruct((count, out_dim), jnp.bfloat16)] * 2,
        in_specs=[pl.BlockSpec(memory_space=pltpu.SMEM), pl.BlockSpec(memory_space=pltpu.VMEM)]
        + [pl.BlockSpec(memory_space=pl.ANY)] * 4,
        out_specs=[pl.BlockSpec(memory_space=pltpu.VMEM)] * 2,
        scratch_shapes=[
            pltpu.VMEM((count, width), jnp.bfloat16),
            pltpu.VMEM((4, depth, out_dim), jnp.bfloat16),
            pltpu.SemaphoreType.DMA((4,)),
        ],
        compiler_params=pltpu.CompilerParams(vmem_limit_bytes=24 << 20),
        cost_estimate=pl.CostEstimate(flops=3760000000, bytes_accessed=12000000, transcendentals=262144),
    )(expert.reshape(1).astype(jnp.int32), codes, *weights)


def interleave_kernel(core_ref, own_ref, other_ref, out_ref, staged, ordered, *, n_y, per_group):
    rows = own_ref.shape[0]
    in_block = rows // n_y
    n_group = in_block // per_group
    per_source = 2 * n_y * per_group
    tiles = own_ref.shape[1] // LANES

    def place(ref, core):
        for lane in range(tiles):
            staged[lane] = ref[:, lane * LANES : (lane + 1) * LANES].astype(jnp.float32)
        for lane in range(tiles):
            for y in range(n_y):
                for i in range(per_group):
                    to = pl.ds((2 * y + core) * per_group + i, n_group, stride=per_source)
                    ordered[lane, to, :] = staged[lane, pl.ds(y * in_block + i, n_group, stride=per_group), :]

    for core in range(2):

        @pl.when(core_ref[0] == core)
        def _():
            place(own_ref, core)
            place(other_ref, 1 - core)

    for lane in range(tiles):
        out_ref[:, lane * LANES : (lane + 1) * LANES] = ordered[lane].astype(out_ref.dtype)


def interleave(core, own, other, n_y, per_group):
    rows, width = own.shape
    return pl.pallas_call(
        functools.partial(interleave_kernel, n_y=n_y, per_group=per_group),
        out_shape=jax.ShapeDtypeStruct((2 * rows, width), own.dtype),
        in_specs=[pl.BlockSpec(memory_space=pltpu.SMEM)] + [pl.BlockSpec(memory_space=pltpu.VMEM)] * 2,
        out_specs=pl.BlockSpec(memory_space=pltpu.VMEM),
        scratch_shapes=[
            pltpu.VMEM((width // LANES, rows, LANES), jnp.float32),
            pltpu.VMEM((width // LANES, 2 * rows, LANES), jnp.float32),
        ],
        compiler_params=pltpu.CompilerParams(vmem_limit_bytes=8 << 20),
    )(core.reshape(1).astype(jnp.int32), own, other)


def shards(tokens, routes, route_gates, gate_weight, up_weight):
    n_group = lax.axis_size("group")
    n_local = lax.axis_size("local")
    n_y = n_local // 2
    width = tokens.shape[1]
    experts = n_group * EXP_MESH
    per_group = tokens.shape[0] // BLOCK
    local = lax.axis_index("local")
    core = local % 2
    my_expert = lax.axis_index("group") * EXP_MESH + local // (n_local // EXP_MESH)
    swap = [(2 * y + c, 2 * y + 1 - c) for y in range(n_y) for c in range(2)]
    same_core = [[2 * y + c for y in range(n_y)] for c in range(2)]

    packed = pack_rows(tokens, routes, route_gates, n_group, experts)
    received = lax.all_to_all(packed, "group", split_axis=0, concat_axis=0, tiled=True)
    other_gate = lax.ppermute(gate_weight, "local", swap)
    other_up = lax.ppermute(up_weight, "local", swap)
    received, other_gate, other_up = lax.optimization_barrier((received, other_gate, other_up))
    received = received.reshape(1, n_group * per_group, width + experts)
    gathered = lax.all_gather(received, "local", axis=0, axis_index_groups=same_core, tiled=True)
    gathered = gathered.reshape(-1, width + experts)

    for_other, own = multiply(my_expert, gathered, width, (other_gate[0], other_up[0], gate_weight[0], up_weight[0]))
    from_other = lax.ppermute(for_other, "local", swap)
    out = interleave(core, own, from_other, n_y, per_group)
    return out.reshape((1,) + out.shape)


def solution(mesh):
    placed = (
        P(("group", "local"), None),
        P(("group", "local"), None),
        P(("group", "local"), None),
        P(("group", "local"), None, None),
        P(("group", "local"), None, None),
    )
    return jax.shard_map(
        shards,
        mesh=mesh,
        in_specs=placed,
        out_specs=P(("group", "local"), None, None),
        check_vma=False,
    )
```

time: 89.1 us -> 93.3 us (1.047)
  Pallas kernels: 2.18 us -> 13.9 us
  matrix products: 8.28 us -> 0 us
  waiting for transfers between devices: 8.4 us -> 14.7 us
  local copies, waits for them, and re-layouts: 4.09 us -> 0.21 us
  other arithmetic: 1.01 us -> 0 us
    pallas_call x1 -> x3, Pallas kernels: 2.18 us -> 13.9 us  [the longest x1 9.73 us: multiply(): pl.pallas_call(hidden_kernel, out_shape=[jax.ShapeDtypeStruct((count, out...]
    dot_general x4 -> x0, matrix products: 8.28 us -> none  [the longest x2 4.27 us: hidden(): pre_up = jnp.dot(rows, up[0], preferred_element_type=jnp.float32) * scale]
    all_to_all x1, starting transfers between devices: 13.7 us -> 7.54 us  [shards(): lax.all_to_all(packed, 'group', split_axis=0, concat_axis=0, tiled=True)]
    ppermute x1, starting transfers between devices: 2.87 us -> 8.74 us  [shards(): other_gate = lax.ppermute(gate_weight, 'local', swap)]
    all_to_all x1, waiting for transfers between devices: 8.39 us -> 13.6 us  [shards(): lax.all_to_all(packed, 'group', split_axis=0, concat_axis=0, tiled=True)]
    reshape x4 -> x0, local copies, waits for them, and re-layouts: 3.34 us -> none  [the longest x1 2.14 us: shards(): packed = packed.reshape(n_group, per_group, width + experts)]
    ppermute x1, waiting for transfers between devices: 0.01 us -> 1.13 us  [shards(): from_other = lax.ppermute(for_other, 'local', swap)]
  transfers between devices with their start and end apart: 4 -> 4, of which waited for: 1 -> 2; matrix products, arithmetic and copies ran while one was open for 7% -> 0% of each run, Pallas kernels for 0% -> 2%
where the time goes in v2:
time: 93.3 us; the launch traced here: 92.9 us
  blocking collectives  39.7 us (43%)
  starting transfers between devices  24.3 us (26%)
  waiting for transfers between devices  14.7 us (16%)
  Pallas kernels  13.9 us (15%)
    all_gather x1, blocking collectives, shards(): lax.all_gather(received, 'local', axis=0, axis_index_groups=same_core, ti...  39.7 us
    all_to_all x1, waiting for transfers between devices, shards(): lax.all_to_all(packed, 'group', split_axis=0, concat_axis=0, tiled=True)  13.6 us
    pallas_call x1, Pallas kernels, multiply(): pl.pallas_call(hidden_kernel, out_shape=[jax.ShapeDtypeStruct((count, out...  9.73 us
    ppermute x1, starting transfers between devices, shards(): other_gate = lax.ppermute(gate_weight, 'local', swap)  8.74 us
    all_to_all x1, starting transfers between devices, shards(): lax.all_to_all(packed, 'group', split_axis=0, concat_axis=0, tiled=True)  7.54 us
    ppermute x1, starting transfers between devices, shards(): from_other = lax.ppermute(for_other, 'local', swap)  6.09 us
    pallas_call x1, Pallas kernels, pack_rows(): pl.pallas_call(pack_kernel, out_shape=jax.ShapeDtypeStruct((n_group, coun...  2.2 us
    pallas_call x1, Pallas kernels, interleave(): pl.pallas_call(functools.partial(interleave_kernel, n_y=n_y, per_group=pe...  1.93 us
  transfers between devices with their start and end apart: 4, of which 2 were waited for; matrix products, arithmetic and copies ran while one was open for 0% of the time, Pallas kernels for 2%

profile of v2, /device:TPU:1, one launch (start us, length us, event | category | flops | bytes accessed | tf_op | source)
XLA Modules:
  0.0 92.9 jit_solution(17340064953084080538)
XLA Ops:
  0.0 8.7 %collective-permute-start = (bf16[1,3584,256]{2,1,0:T(8,128)(2,1)}, bf16[1,3584,256]{2,1,0:T(8,128)(2,1)S(1)}, u32[]{:S(2)}, u32[]{:S(2)}) collective-permute-start(bf16[1,3584,256]{2,1,0:T(8,128)(2,1)} %param.8), channel_id=1, source_target_pairs={{0,1},{1,0},{2,3},{3,2},{4,5},{5,4},{6,7},{7,6},{8,9},{9,8},{10,11... | collective-permute-start | bytes 5505032 | tf_op jit(solution)/shard_map/ppermute | solution.py:161
  8.7 1.9 %collective-permute-start.1 = (bf16[1,3584,256]{2,1,0:T(8,128)(2,1)}, bf16[1,3584,256]{2,1,0:T(8,128)(2,1)}, u32[]{:S(2)}, u32[]{:S(2)}) collective-permute-start(bf16[1,3584,256]{2,1,0:T(8,128)(2,1)} %param.9), channel_id=1, source_target_pairs={{0,1},{1,0},{2,3},{3,2},{4,5},{5,4},{6,7},{7,6},{8,9},{9,8},{10,11... | collective-permute-start | bytes 5505032 | tf_op jit(solution)/shard_map/ppermute | solution.py:162
  10.7 2.2 %shard_map.55 = s16[32,2,3712]{2,1,0:T(2,128)(2,1)} custom-call(bf16[8,3584]{1,0:T(8,128)(2,1)} %tokens_ref.1, s32[8,8]{1,0:T(8,128)} %routes_ref.1, f32[8,8]{1,0:T(8,128)} %gates_ref.1), custom_call_target="tpu_custom_call" | custom-call | tf_op jit(solution)/shard_map/pallas_call | solution.py:57
  12.9 7.5 %all-to-all-start = ((s16[32,2,3712]{2,1,0:T(2,128)(2,1)}), s16[32,2,3712]{2,1,0:T(2,128)(2,1)S(1)}, u32[]{:S(2)}, u32[]{:S(2)}) async-start(s16[32,2,3712]{2,1,0:T(2,128)(2,1)} %shard_map.55), calls=%async_computation | async-start | bytes 950272 | tf_op jit(solution)/shard_map/all_to_all | solution.py:160
  20.4 13.6 %all-to-all-done = s16[32,2,3712]{2,1,0:T(2,128)(2,1)S(1)} async-done(((s16[32,2,3712]{2,1,0:T(2,128)(2,1)}), s16[32,2,3712]{2,1,0:T(2,128)(2,1)S(1)}, u32[]{:S(2)}, u32[]{:S(2)}) %all-to-all-start) | async-done | bytes 475168 | tf_op jit(solution)/shard_map/all_to_all | solution.py:160
  34.0 0.0 collective-permute-done
  34.0 0.0 collective-permute-done.1
  34.0 0.2 reshape.17
  34.2 0.0 copy-start
  34.2 0.0 copy-start.1
  34.2 39.7 %all-gather.1 = s16[8,64,3712]{2,1,0:T(8,128)(2,1)S(1)} all-gather(s16[1,64,3712]{2,1,0:T(8,128)(2,1)S(1)} %reshape.17), channel_id=1, replica_groups={{0,2,4,6,8,10,12,14},{1,3,5,7,9,11,13,15},{16,18,20,22,24,26,28,30},{17..., dimensions={0}, use_global_device_ids=true | all-gather | bytes 4276224 | tf_op jit(solution)/shard_map/all_gather | solution.py:165
  74.0 0.0 copy-done
  74.0 0.0 copy-done.1
  74.0 9.7 %shard_map.56 = (bf16[512,256]{1,0:T(8,128)(2,1)S(1)}, bf16[512,256]{1,0:T(8,128)(2,1)S(1)}) custom-call(s32[1]{0:T(128)} %bitcast.1.expert_ref, s16[512,3712]{1,0:T(8,128)(2,1)S(1)} %bitcast.8, bf16[3584,256]{1,0:T(8,128)(2,1)S(1)} %bitcast.11, bf16[3584,256]{1,0:T(8,128)(2,1)} %bitcast.4.refs_1_, bf16[3584,256]{1,0:T(8,128)(2,1)S(1)} %bitcast.9, ...), custom_call_target="tpu_custom_call" | custom-call | flops 3760000000 | bytes 12000000 | tf_op jit(solution)/shard_map/pallas_call | solution.py:88
  83.7 6.1 %collective-permute-start.2 = (bf16[512,256]{1,0:T(8,128)(2,1)S(1)}, bf16[512,256]{1,0:T(8,128)(2,1)S(1)}, u32[]{:S(2)}, u32[]{:S(2)}) collective-permute-start(bf16[512,256]{1,0:T(8,128)(2,1)S(1)} %get-tuple-element.14), channel_id=1, source_target_pairs={{0,1},{1,0},{2,3},{3,2},{4,5},{5,4},{6,7},{7,6},{8,9},{9,8},{10,11... | collective-permute-start | bytes 786440 | tf_op jit(solution)/shard_map/ppermute | solution.py:169
  89.8 1.1 %collective-permute-done.2.other_ref = bf16[512,256]{1,0:T(8,128)(2,1)S(1)} collective-permute-done((bf16[512,256]{1,0:T(8,128)(2,1)S(1)}, bf16[512,256]{1,0:T(8,128)(2,1)S(1)}, u32[]{:S(2)}, u32[]{:S(2)}) %collective-permute-start.2) | collective-permute-done | bytes 262176 | tf_op jit(solution)/shard_map/ppermute | solution.py:169
  91.0 1.9 %shard_map.57 = bf16[1024,256]{1,0:T(8,128)(2,1)} custom-call(s32[1]{0:T(128)} %bitcast.core_ref, bf16[512,256]{1,0:T(8,128)(2,1)S(1)} %get-tuple-element.13.own_ref, bf16[512,256]{1,0:T(8,128)(2,1)S(1)} %collective-permute-done.2.other_ref), custom_call_target="tpu_custom_call" | custom-call | tf_op jit(solution)/shard_map/pallas_call | solution.py:133
Async XLA Ops:
  0.0 34.0 %collective-permute-start = (bf16[1,3584,256]{2,1,0:T(8,128)(2,1)}, bf16[1,3584,256]{2,1,0:T(8,128)(2,1)S(1)}, u32[]{:S(2)}, u32[]{:S(2)}) collective-permute-start(bf16[1,3584,256]{2,1,0:T(8,128)(2,1)} %param.8), channel_id=1, source_target_pairs={{0,1},{1,0},{2,3},{3,2},{4,5},{5,4},{6,7},{7,6},{8,9},{9,8},{10,11... | collective-permute-start | bytes 5505032 | tf_op jit(solution)/shard_map/ppermute | solution.py:161
  8.7 25.3 %collective-permute-start.1 = (bf16[1,3584,256]{2,1,0:T(8,128)(2,1)}, bf16[1,3584,256]{2,1,0:T(8,128)(2,1)}, u32[]{:S(2)}, u32[]{:S(2)}) collective-permute-start(bf16[1,3584,256]{2,1,0:T(8,128)(2,1)} %param.9), channel_id=1, source_target_pairs={{0,1},{1,0},{2,3},{3,2},{4,5},{5,4},{6,7},{7,6},{8,9},{9,8},{10,11... | collective-permute-start | bytes 5505032 | tf_op jit(solution)/shard_map/ppermute | solution.py:162
  12.9 21.1 %all-to-all-start = ((s16[32,2,3712]{2,1,0:T(2,128)(2,1)}), s16[32,2,3712]{2,1,0:T(2,128)(2,1)S(1)}, u32[]{:S(2)}, u32[]{:S(2)}) async-start(s16[32,2,3712]{2,1,0:T(2,128)(2,1)} %shard_map.55), calls=%async_computation | async-start | bytes 950272 | tf_op jit(solution)/shard_map/all_to_all | solution.py:160
  34.2 39.8 %copy-start = (bf16[1,3584,256]{2,1,0:T(8,128)(2,1)S(1)}, bf16[1,3584,256]{2,1,0:T(8,128)(2,1)}, u32[]{:S(2)}) copy-start(bf16[1,3584,256]{2,1,0:T(8,128)(2,1)} %param.8) | copy-start | bytes 5505028
  34.2 39.8 %copy-start.1 = (bf16[1,3584,256]{2,1,0:T(8,128)(2,1)S(1)}, bf16[1,3584,256]{2,1,0:T(8,128)(2,1)}, u32[]{:S(2)}) copy-start(bf16[1,3584,256]{2,1,0:T(8,128)(2,1)} %param.9) | copy-start | bytes 5505028
  83.7 7.2 %collective-permute-start.2 = (bf16[512,256]{1,0:T(8,128)(2,1)S(1)}, bf16[512,256]{1,0:T(8,128)(2,1)S(1)}, u32[]{:S(2)}, u32[]{:S(2)}) collective-permute-start(bf16[512,256]{1,0:T(8,128)(2,1)S(1)} %get-tuple-element.14), channel_id=1, source_target_pairs={{0,1},{1,0},{2,3},{3,2},{4,5},{5,4},{6,7},{7,6},{8,9},{9,8},{10,11... | collective-permute-start | bytes 786440 | tf_op jit(solution)/shard_map/ppermute | solution.py:169

commit v3 on v2

v3 whole, which is shorter than its diff:
```python
import functools

import jax
import jax.numpy as jnp
from jax import lax
from jax.experimental import pallas as pl
from jax.experimental.pallas import tpu as pltpu
from jax.sharding import PartitionSpec as P

EXP_MESH = 4
BLOCK = 4
LANES = 128
CHUNKS = 4
GATE_ONE = 16000.0
CODE_MAX = 32000.0
EXP_BIAS = 200.0


def pack_kernel(tokens_ref, routes_ref, gates_ref, out_ref):
    count, width = tokens_ref.shape
    n_group, per_group, packed_width = out_ref.shape
    rows = n_group * per_group
    experts = packed_width - width
    tok = tokens_ref[...].astype(jnp.float32)
    largest = jnp.maximum(jnp.max(jnp.abs(tok), axis=1, keepdims=True), 1e-25)
    power = jnp.floor(jnp.log2(CODE_MAX / largest))
    codes = jnp.round(tok * jnp.exp2(power))
    routes = routes_ref[...]
    gate_codes = jnp.round(gates_ref[...] * GATE_ONE)
    expert = lax.broadcasted_iota(jnp.int32, (count, experts), 1)
    row = lax.broadcasted_iota(jnp.int32, (count, rows), 1)
    token = lax.broadcasted_iota(jnp.int32, (count, rows), 0)
    side = jnp.zeros((count, experts), jnp.float32)
    chosen = jnp.zeros((count, rows), jnp.float32)
    for k in range(routes.shape[1]):
        route = routes[:, k : k + 1]
        side = side + jnp.where(expert == route, gate_codes[:, k : k + 1], 0.0)
        chosen = jnp.where(route // EXP_MESH == row // per_group, 1.0, chosen)
    side = jnp.where(side > 0.0, side, -(power + EXP_BIAS))
    chosen = jnp.where(token // BLOCK == row % per_group, chosen, 0.0)
    chosen = chosen.T.astype(jnp.bfloat16)

    def send(values, first, size):
        high = jnp.floor(values * (1.0 / 256.0))
        low = values - 256.0 * high
        picked = jnp.dot(chosen, (256.0 * high).astype(jnp.bfloat16), preferred_element_type=jnp.float32)
        picked += jnp.dot(chosen, low.astype(jnp.bfloat16), preferred_element_type=jnp.float32)
        picked = picked.astype(jnp.int32).astype(jnp.int16)
        for group in range(n_group):
            out_ref[group, :, first : first + size] = picked[group * per_group : (group + 1) * per_group]

    send(codes, 0, width)
    send(side, width, experts)


def pack_rows(tokens, routes, route_gates, n_group, experts):
    count, width = tokens.shape
    return pl.pallas_call(
        pack_kernel,
        out_shape=jax.ShapeDtypeStruct((n_group, count // BLOCK, width + experts), jnp.int16),
        in_specs=[pl.BlockSpec(memory_space=pltpu.VMEM)] * 3,
        out_specs=pl.BlockSpec(memory_space=pltpu.VMEM),
    )(tokens, routes, route_gates)


def hidden_kernel(codes_ref, gate_ref, up_ref, out_ref, rows, held_up, arrived):
    width = rows.shape[1]
    copy = pltpu.make_async_copy(up_ref, held_up, arrived)
    copy.start()
    expert = lax.axis_index("group") * EXP_MESH + lax.axis_index("local") // (lax.axis_size("local") // EXP_MESH)
    rows[...] = codes_ref[:, :width].astype(jnp.float32).astype(jnp.bfloat16)
    side = codes_ref[:, width:].astype(jnp.float32)
    lane = lax.broadcasted_iota(jnp.int32, side.shape, 1)
    weight = jnp.sum(jnp.where(lane == expert, jnp.maximum(side, 0.0), 0.0), axis=1, keepdims=True)
    weight = weight * (1.0 / GATE_ONE)
    scale = jnp.exp2(jnp.min(side, axis=1, keepdims=True) + EXP_BIAS)
    pre_gate = jnp.dot(rows[...], gate_ref[...], preferred_element_type=jnp.float32) * scale
    copy.wait()
    pre_up = jnp.dot(rows[...], held_up[...], preferred_element_type=jnp.float32) * scale
    out_ref[...] = (pre_gate / (1.0 + jnp.exp(-pre_gate)) * pre_up * weight).astype(out_ref.dtype)


def hidden(codes, width, gate, up):
    count = codes.shape[0]
    out_dim = gate.shape[1]
    return pl.pallas_call(
        hidden_kernel,
        out_shape=jax.ShapeDtypeStruct((count, out_dim), jnp.bfloat16),
        in_specs=[pl.BlockSpec(memory_space=pltpu.VMEM)] * 2 + [pl.BlockSpec(memory_space=pl.ANY)],
        out_specs=pl.BlockSpec(memory_space=pltpu.VMEM),
        scratch_shapes=[
            pltpu.VMEM((count, width), jnp.bfloat16),
            pltpu.VMEM(up.shape, up.dtype),
            pltpu.SemaphoreType.DMA,
        ],
        compiler_params=pltpu.CompilerParams(vmem_limit_bytes=16 << 20),
        cost_estimate=pl.CostEstimate(flops=1880000000, bytes_accessed=8000000, transcendentals=131072),
    )(codes, gate, up)


def interleave_kernel(own_ref, other_ref, out_ref, staged, ordered, done, sent, *, n_y, per_group):
    in_block = own_ref.shape[0] // n_y
    n_group = in_block // per_group
    per_source = 2 * n_y * per_group
    tiles = own_ref.shape[1] // LANES
    my_core = lax.axis_index("local") % 2
    for lane in range(tiles):
        cols = slice(lane * LANES, (lane + 1) * LANES)
        staged[lane, 0] = own_ref[:, cols].astype(jnp.float32)
        staged[lane, 1] = other_ref[:, cols].astype(jnp.float32)
    groups = n_group // CHUNKS
    copies = []
    for chunk in range(CHUNKS):
        for core in range(2):

            @pl.when(my_core == core)
            def _():
                for lane in range(tiles):
                    for y in range(n_y):
                        for i in range(per_group):
                            start = y * in_block + chunk * groups * per_group + i
                            origin = pl.ds(start, groups, stride=per_group)
                            for source in range(2):
                                place = core if source == 0 else 1 - core
                                target = chunk * groups * per_source + (2 * y + place) * per_group + i
                                ordered[lane, pl.ds(target, groups, stride=per_source), :] = staged[
                                    lane, source, origin, :
                                ]

        rows = slice(chunk * groups * per_source, (chunk + 1) * groups * per_source)
        for lane in range(tiles):
            done[rows, lane * LANES : (lane + 1) * LANES] = ordered[lane, rows].astype(done.dtype)
        copy = pltpu.make_async_copy(done.at[rows], out_ref.at[rows], sent.at[chunk])
        copy.start()
        copies.append(copy)
    for copy in copies:
        copy.wait()


def interleave(own, other, n_y, per_group):
    rows, width = own.shape
    tiles = width // LANES
    return pl.pallas_call(
        functools.partial(interleave_kernel, n_y=n_y, per_group=per_group),
        out_shape=jax.ShapeDtypeStruct((2 * rows, width), own.dtype),
        in_specs=[pl.BlockSpec(memory_space=pltpu.VMEM)] * 2,
        out_specs=pl.BlockSpec(memory_space=pl.ANY),
        scratch_shapes=[
            pltpu.VMEM((tiles, 2, rows, LANES), jnp.float32),
            pltpu.VMEM((tiles, 2 * rows, LANES), jnp.float32),
            pltpu.VMEM((2 * rows, width), own.dtype),
            pltpu.SemaphoreType.DMA((CHUNKS,)),
        ],
        compiler_params=pltpu.CompilerParams(vmem_limit_bytes=8 << 20),
        cost_estimate=pl.CostEstimate(flops=0, bytes_accessed=1000000, transcendentals=0),
    )(own, other)


def shards(tokens, routes, route_gates, gate_weight, up_weight):
    n_group = lax.axis_size("group")
    n_local = lax.axis_size("local")
    n_y = n_local // 2
    width = tokens.shape[1]
    experts = n_group * EXP_MESH
    per_group = tokens.shape[0] // BLOCK
    swap = [(2 * y + c, 2 * y + 1 - c) for y in range(n_y) for c in range(2)]
    same_core = [[2 * y + c for y in range(n_y)] for c in range(2)]

    packed = pack_rows(tokens, routes, route_gates, n_group, experts)
    received = lax.all_to_all(packed, "group", split_axis=0, concat_axis=0, tiled=True)
    other_gate = lax.ppermute(gate_weight, "local", swap)
    other_up = lax.ppermute(up_weight, "local", swap)
    received, other_gate, other_up = lax.optimization_barrier((received, other_gate, other_up))
    received = received.reshape(1, n_group * per_group, width + experts)
    gathered = lax.all_gather(received, "local", axis=0, axis_index_groups=same_core, tiled=True)
    gathered = gathered.reshape(-1, width + experts)

    for_other = hidden(gathered, width, other_gate[0], other_up[0])
    from_other = lax.ppermute(for_other, "local", swap)
    own = hidden(gathered, width, gate_weight[0], up_weight[0])
    out = interleave(own, from_other, n_y, per_group)
    return out.reshape((1,) + out.shape)


def solution(mesh):
    placed = (
        P(("group", "local"), None),
        P(("group", "local"), None),
        P(("group", "local"), None),
        P(("group", "local"), None, None),
        P(("group", "local"), None, None),
    )
    return jax.shard_map(
        shards,
        mesh=mesh,
        in_specs=placed,
        out_specs=P(("group", "local"), None, None),
        check_vma=False,
    )
```

time: 93.3 us -> 91.6 us (0.982)
  blocking collectives: 39.7 us -> 60.7 us
  waiting for transfers between devices: 14.7 us -> 0.01 us
  starting transfers between devices: 24.3 us -> 16.8 us
    all_to_all x0 -> x1, blocking collectives: none -> 21.1 us  [shards(): lax.all_to_all(packed, 'group', split_axis=0, concat_axis=0, tiled=True)]
    all_to_all x1 -> x0, waiting for transfers between devices: 13.6 us -> none  [shards(): lax.all_to_all(packed, 'group', split_axis=0, concat_axis=0, tiled=True)]
    all_to_all x1 -> x0, starting transfers between devices: 7.54 us -> none  [shards(): lax.all_to_all(packed, 'group', split_axis=0, concat_axis=0, tiled=True)]
    ppermute x1, waiting for transfers between devices: 1.13 us -> 0.01 us  [shards(): from_other = lax.ppermute(for_other, 'local', swap)]
    pallas_call x1 -> x2, Pallas kernels: 9.73 us -> 9.69 us  [hidden(): pl.pallas_call(hidden_kernel, out_shape=jax.ShapeDtypeStruct((count, out_...]
  transfers between devices with their start and end apart: 4 -> 3, of which waited for: 2 -> 0; matrix products, arithmetic and copies ran while one was open for 0% -> 0% of each run, Pallas kernels for 2% -> 7%
where the time goes in v3:
time: 91.6 us; the launch traced here: 91.2 us
  blocking collectives  60.7 us (66%)
  starting transfers between devices  16.8 us (18%)
  Pallas kernels  13.4 us (15%)
    all_gather x1, blocking collectives, shards(): lax.all_gather(received, 'local', axis=0, axis_index_groups=same_core, ti...  39.6 us
    all_to_all x1, blocking collectives, shards(): lax.all_to_all(packed, 'group', split_axis=0, concat_axis=0, tiled=True)  21.1 us
    pallas_call x2, Pallas kernels, hidden(): pl.pallas_call(hidden_kernel, out_shape=jax.ShapeDtypeStruct((count, out_...  9.69 us
    ppermute x1, starting transfers between devices, shards(): other_gate = lax.ppermute(gate_weight, 'local', swap)  8.74 us
    ppermute x1, starting transfers between devices, shards(): from_other = lax.ppermute(for_other, 'local', swap)  6.09 us
    pallas_call x1, Pallas kernels, pack_rows(): pl.pallas_call(pack_kernel, out_shape=jax.ShapeDtypeStruct((n_group, coun...  2.2 us
    ppermute x1, starting transfers between devices, shards(): other_up = lax.ppermute(up_weight, 'local', swap)  1.92 us
  transfers between devices with their start and end apart: 3, of which 0 were waited for; matrix products, arithmetic and copies ran while one was open for 0% of the time, Pallas kernels for 7%

profile of v3, /device:TPU:1, one launch (start us, length us, event | category | flops | bytes accessed | tf_op | source)
XLA Modules:
  0.0 91.2 jit_solution(4252246990903565396)
XLA Ops:
  0.0 8.7 %collective-permute-start = (bf16[1,3584,256]{2,1,0:T(8,128)(2,1)}, bf16[1,3584,256]{2,1,0:T(8,128)(2,1)S(1)}, u32[]{:S(2)}, u32[]{:S(2)}) collective-permute-start(bf16[1,3584,256]{2,1,0:T(8,128)(2,1)} %param.8), channel_id=1, source_target_pairs={{0,1},{1,0},{2,3},{3,2},{4,5},{5,4},{6,7},{7,6},{8,9},{9,8},{10,11... | collective-permute-start | bytes 5505032 | tf_op jit(solution)/shard_map/ppermute | solution.py:171
  8.7 1.9 %collective-permute-start.1 = (bf16[1,3584,256]{2,1,0:T(8,128)(2,1)}, bf16[1,3584,256]{2,1,0:T(8,128)(2,1)}, u32[]{:S(2)}, u32[]{:S(2)}) collective-permute-start(bf16[1,3584,256]{2,1,0:T(8,128)(2,1)} %param.9), channel_id=1, source_target_pairs={{0,1},{1,0},{2,3},{3,2},{4,5},{5,4},{6,7},{7,6},{8,9},{9,8},{10,11... | collective-permute-start | bytes 5505032 | tf_op jit(solution)/shard_map/ppermute | solution.py:172
  10.7 2.2 %shard_map.55 = s16[32,2,3712]{2,1,0:T(2,128)(2,1)} custom-call(bf16[8,3584]{1,0:T(8,128)(2,1)} %tokens_ref.1, s32[8,8]{1,0:T(8,128)} %routes_ref.1, f32[8,8]{1,0:T(8,128)} %gates_ref.1), custom_call_target="tpu_custom_call" | custom-call | tf_op jit(solution)/shard_map/pallas_call | solution.py:58
  12.9 21.1 %all_to_all.5 = s16[32,2,3712]{2,1,0:T(2,128)(2,1)S(1)} all-to-all(s16[32,2,3712]{2,1,0:T(2,128)(2,1)} %shard_map.55), channel_id=1, replica_groups=mesh['group'=32,'local'=16] {'group'}, dimensions={0} | all-to-all | bytes 950272 | tf_op jit(solution)/shard_map/all_to_all | solution.py:170
  34.0 0.0 collective-permute-done
  34.0 0.0 collective-permute-done.1
  34.0 0.2 reshape.9
  34.2 39.6 %all-gather.1 = s16[8,64,3712]{2,1,0:T(8,128)(2,1)S(1)} all-gather(s16[1,64,3712]{2,1,0:T(8,128)(2,1)S(1)} %reshape.9), channel_id=1, replica_groups={{0,2,4,6,8,10,12,14},{1,3,5,7,9,11,13,15},{16,18,20,22,24,26,28,30},{17..., dimensions={0}, use_global_device_ids=true | all-gather | bytes 4276224 | tf_op jit(solution)/shard_map/all_gather | solution.py:175
  73.8 0.0 copy-start
  73.8 0.0 copy-start.1
  73.8 5.5 %shard_map.57 = bf16[512,256]{1,0:T(8,128)(2,1)S(1)} custom-call(s16[512,3712]{1,0:T(8,128)(2,1)S(1)} %bitcast.6, bf16[3584,256]{1,0:T(8,128)(2,1)S(1)} %bitcast.10, bf16[3584,256]{1,0:T(8,128)(2,1)} %bitcast.4.up_ref), custom_call_target="tpu_custom_call" | custom-call | flops 1880000000 | bytes 8000000 | tf_op jit(solution)/shard_map/pallas_call | solution.py:86
  79.3 6.1 %collective-permute-start.2 = (bf16[512,256]{1,0:T(8,128)(2,1)S(1)}, bf16[512,256]{1,0:T(8,128)(2,1)S(1)}, u32[]{:S(2)}, u32[]{:S(2)}) collective-permute-start(bf16[512,256]{1,0:T(8,128)(2,1)S(1)} %shard_map.57), channel_id=1, source_target_pairs={{0,1},{1,0},{2,3},{3,2},{4,5},{5,4},{6,7},{7,6},{8,9},{9,8},{10,11... | collective-permute-start | bytes 786440 | tf_op jit(solution)/shard_map/ppermute | solution.py:179
  85.4 0.0 copy-done
  85.4 0.0 copy-done.1
  85.4 4.2 %shard_map.56.own_ref = bf16[512,256]{1,0:T(8,128)(2,1)S(1)} custom-call(s16[512,3712]{1,0:T(8,128)(2,1)S(1)} %bitcast.7, bf16[3584,256]{1,0:T(8,128)(2,1)S(1)} %bitcast.8, bf16[3584,256]{1,0:T(8,128)(2,1)S(1)} %bitcast.9), custom_call_target="tpu_custom_call" | custom-call | flops 1880000000 | bytes 8000000 | tf_op jit(solution)/shard_map/pallas_call | solution.py:86
  89.6 0.0 collective-permute-done.2.other_ref
  89.7 1.5 %shard_map.58 = bf16[1024,256]{1,0:T(8,128)(2,1)} custom-call(bf16[512,256]{1,0:T(8,128)(2,1)S(1)} %shard_map.56.own_ref, bf16[512,256]{1,0:T(8,128)(2,1)S(1)} %collective-permute-done.2.other_ref), custom_call_target="tpu_custom_call" | custom-call | bytes 1000000 | tf_op jit(solution)/shard_map/pallas_call | solution.py:143
Async XLA Ops:
  0.0 34.0 %collective-permute-start = (bf16[1,3584,256]{2,1,0:T(8,128)(2,1)}, bf16[1,3584,256]{2,1,0:T(8,128)(2,1)S(1)}, u32[]{:S(2)}, u32[]{:S(2)}) collective-permute-start(bf16[1,3584,256]{2,1,0:T(8,128)(2,1)} %param.8), channel_id=1, source_target_pairs={{0,1},{1,0},{2,3},{3,2},{4,5},{5,4},{6,7},{7,6},{8,9},{9,8},{10,11... | collective-permute-start | bytes 5505032 | tf_op jit(solution)/shard_map/ppermute | solution.py:171
  8.7 25.3 %collective-permute-start.1 = (bf16[1,3584,256]{2,1,0:T(8,128)(2,1)}, bf16[1,3584,256]{2,1,0:T(8,128)(2,1)}, u32[]{:S(2)}, u32[]{:S(2)}) collective-permute-start(bf16[1,3584,256]{2,1,0:T(8,128)(2,1)} %param.9), channel_id=1, source_target_pairs={{0,1},{1,0},{2,3},{3,2},{4,5},{5,4},{6,7},{7,6},{8,9},{9,8},{10,11... | collective-permute-start | bytes 5505032 | tf_op jit(solution)/shard_map/ppermute | solution.py:172
  73.8 11.6 %copy-start = (bf16[1,3584,256]{2,1,0:T(8,128)(2,1)S(1)}, bf16[1,3584,256]{2,1,0:T(8,128)(2,1)}, u32[]{:S(2)}) copy-start(bf16[1,3584,256]{2,1,0:T(8,128)(2,1)} %param.8) | copy-start | bytes 5505028
  73.8 11.6 %copy-start.1 = (bf16[1,3584,256]{2,1,0:T(8,128)(2,1)S(1)}, bf16[1,3584,256]{2,1,0:T(8,128)(2,1)}, u32[]{:S(2)}) copy-start(bf16[1,3584,256]{2,1,0:T(8,128)(2,1)} %param.9) | copy-start | bytes 5505028
  79.3 10.4 %collective-permute-start.2 = (bf16[512,256]{1,0:T(8,128)(2,1)S(1)}, bf16[512,256]{1,0:T(8,128)(2,1)S(1)}, u32[]{:S(2)}, u32[]{:S(2)}) collective-permute-start(bf16[512,256]{1,0:T(8,128)(2,1)S(1)} %shard_map.57), channel_id=1, source_target_pairs={{0,1},{1,0},{2,3},{3,2},{4,5},{5,4},{6,7},{7,6},{8,9},{9,8},{10,11... | collective-permute-start | bytes 786440 | tf_op jit(solution)/shard_map/ppermute | solution.py:179

commit v4 on v3

--- a/solution.py
+++ b/solution.py
@@ -63,9 +63,9 @@
     )(tokens, routes, route_gates)
 
 
-def hidden_kernel(codes_ref, gate_ref, up_ref, out_ref, rows, held_up, arrived):
+def hidden_kernel(codes_ref, gate_ref, up_ref, gate_of_other_ref, up_of_other_ref, own_ref, other_ref, rows, held, arrived):
     width = rows.shape[1]
-    copy = pltpu.make_async_copy(up_ref, held_up, arrived)
+    copy = pltpu.make_async_copy(up_of_other_ref, held, arrived)
     copy.start()
     expert = lax.axis_index("group") * EXP_MESH + lax.axis_index("local") // (lax.axis_size("local") // EXP_MESH)
     rows[...] = codes_ref[:, :width].astype(jnp.float32).astype(jnp.bfloat16)
@@ -74,28 +74,33 @@
     weight = jnp.sum(jnp.where(lane == expert, jnp.maximum(side, 0.0), 0.0), axis=1, keepdims=True)
     weight = weight * (1.0 / GATE_ONE)
     scale = jnp.exp2(jnp.min(side, axis=1, keepdims=True) + EXP_BIAS)
-    pre_gate = jnp.dot(rows[...], gate_ref[...], preferred_element_type=jnp.float32) * scale
+
+    def multiply(gate, up, out_ref):
+        pre_gate = jnp.dot(rows[...], gate[...], preferred_element_type=jnp.float32) * scale
+        pre_up = jnp.dot(rows[...], up[...], preferred_element_type=jnp.float32) * scale
+        out_ref[...] = (pre_gate / (1.0 + jnp.exp(-pre_gate)) * pre_up * weight).astype(out_ref.dtype)
+
+    multiply(gate_ref, up_ref, own_ref)
     copy.wait()
-    pre_up = jnp.dot(rows[...], held_up[...], preferred_element_type=jnp.float32) * scale
-    out_ref[...] = (pre_gate / (1.0 + jnp.exp(-pre_gate)) * pre_up * weight).astype(out_ref.dtype)
-
-
-def hidden(codes, width, gate, up):
+    multiply(gate_of_other_ref, held, other_ref)
+
+
+def hidden(codes, width, weights):
     count = codes.shape[0]
-    out_dim = gate.shape[1]
+    shape = weights[0].shape
     return pl.pallas_call(
         hidden_kernel,
-        out_shape=jax.ShapeDtypeStruct((count, out_dim), jnp.bfloat16),
-        in_specs=[pl.BlockSpec(memory_space=pltpu.VMEM)] * 2 + [pl.BlockSpec(memory_space=pl.ANY)],
-        out_specs=pl.BlockSpec(memory_space=pltpu.VMEM),
+        out_shape=[jax.ShapeDtypeStruct((count, shape[1]), jnp.bfloat16)] * 2,
+        in_specs=[pl.BlockSpec(memory_space=pltpu.VMEM)] * 4 + [pl.BlockSpec(memory_space=pl.ANY)],
+        out_specs=[pl.BlockSpec(memory_space=pltpu.VMEM)] * 2,
         scratch_shapes=[
             pltpu.VMEM((count, width), jnp.bfloat16),
-            pltpu.VMEM(up.shape, up.dtype),
+            pltpu.VMEM(shape, jnp.bfloat16),
             pltpu.SemaphoreType.DMA,
         ],
         compiler_params=pltpu.CompilerParams(vmem_limit_bytes=16 << 20),
-        cost_estimate=pl.CostEstimate(flops=1880000000, bytes_accessed=8000000, transcendentals=131072),
-    )(codes, gate, up)
+        cost_estimate=pl.CostEstimate(flops=3760000000, bytes_accessed=12000000, transcendentals=262144),
+    )(codes, *weights)
 
 
 def interleave_kernel(own_ref, other_ref, out_ref, staged, ordered, done, sent, *, n_y, per_group):
@@ -175,9 +180,8 @@
     gathered = lax.all_gather(received, "local", axis=0, axis_index_groups=same_core, tiled=True)
     gathered = gathered.reshape(-1, width + experts)
 
-    for_other = hidden(gathered, width, other_gate[0], other_up[0])
+    own, for_other = hidden(gathered, width, (gate_weight[0], up_weight[0], other_gate[0], other_up[0]))
     from_other = lax.ppermute(for_other, "local", swap)
-    own = hidden(gathered, width, gate_weight[0], up_weight[0])
     out = interleave(own, from_other, n_y, per_group)
     return out.reshape((1,) + out.shape)
 

time: 91.6 us -> 88.5 us (0.966)
  Pallas kernels: 13.4 us -> 9.05 us
  waiting for transfers between devices: 0.01 us -> 1.15 us
    pallas_call x2 -> x1, Pallas kernels: 9.69 us -> 5.34 us  [hidden(): pl.pallas_call(hidden_kernel, out_shape=[jax.ShapeDtypeStruct((count, sha...]
    ppermute x1, waiting for transfers between devices: 0.01 us -> 1.14 us  [shards(): from_other = lax.ppermute(for_other, 'local', swap)]
  transfers between devices with their start and end apart: 3 -> 3, of which waited for: 0 -> 1; matrix products, arithmetic and copies ran while one was open for 0% -> 0% of each run, Pallas kernels for 7% -> 2%
where the time goes in v4:
time: 88.5 us; the launch traced here: 88.1 us
  blocking collectives  60.9 us (69%)
  starting transfers between devices  16.8 us (19%)
  Pallas kernels  9.05 us (10%)
  waiting for transfers between devices  1.15 us (1%)
    all_gather x1, blocking collectives, shards(): lax.all_gather(received, 'local', axis=0, axis_index_groups=same_core, ti...  39.7 us
    all_to_all x1, blocking collectives, shards(): lax.all_to_all(packed, 'group', split_axis=0, concat_axis=0, tiled=True)  21.1 us
    ppermute x1, starting transfers between devices, shards(): other_gate = lax.ppermute(gate_weight, 'local', swap)  8.74 us
    ppermute x1, starting transfers between devices, shards(): from_other = lax.ppermute(for_other, 'local', swap)  6.09 us
    pallas_call x1, Pallas kernels, hidden(): pl.pallas_call(hidden_kernel, out_shape=[jax.ShapeDtypeStruct((count, sha...  5.34 us
    pallas_call x1, Pallas kernels, pack_rows(): pl.pallas_call(pack_kernel, out_shape=jax.ShapeDtypeStruct((n_group, coun...  2.2 us
    ppermute x1, starting transfers between devices, shards(): other_up = lax.ppermute(up_weight, 'local', swap)  1.92 us
  transfers between devices with their start and end apart: 3, of which 1 were waited for; matrix products, arithmetic and copies ran while one was open for 0% of the time, Pallas kernels for 2%

profile of v4, /device:TPU:1, one launch (start us, length us, event | category | flops | bytes accessed | tf_op | source)
XLA Modules:
  0.0 88.1 jit_solution(1530234045459708291)
XLA Ops:
  0.0 8.7 %collective-permute-start = (bf16[1,3584,256]{2,1,0:T(8,128)(2,1)}, bf16[1,3584,256]{2,1,0:T(8,128)(2,1)S(1)}, u32[]{:S(2)}, u32[]{:S(2)}) collective-permute-start(bf16[1,3584,256]{2,1,0:T(8,128)(2,1)} %param.8), channel_id=1, source_target_pairs={{0,1},{1,0},{2,3},{3,2},{4,5},{5,4},{6,7},{7,6},{8,9},{9,8},{10,11... | collective-permute-start | bytes 5505032 | tf_op jit(solution)/shard_map/ppermute | solution.py:176
  8.7 1.9 %collective-permute-start.1 = (bf16[1,3584,256]{2,1,0:T(8,128)(2,1)}, bf16[1,3584,256]{2,1,0:T(8,128)(2,1)}, u32[]{:S(2)}, u32[]{:S(2)}) collective-permute-start(bf16[1,3584,256]{2,1,0:T(8,128)(2,1)} %param.9), channel_id=1, source_target_pairs={{0,1},{1,0},{2,3},{3,2},{4,5},{5,4},{6,7},{7,6},{8,9},{9,8},{10,11... | collective-permute-start | bytes 5505032 | tf_op jit(solution)/shard_map/ppermute | solution.py:177
  10.7 2.2 %shard_map.55 = s16[32,2,3712]{2,1,0:T(2,128)(2,1)} custom-call(bf16[8,3584]{1,0:T(8,128)(2,1)} %tokens_ref.1, s32[8,8]{1,0:T(8,128)} %routes_ref.1, f32[8,8]{1,0:T(8,128)} %gates_ref.1), custom_call_target="tpu_custom_call" | custom-call | tf_op jit(solution)/shard_map/pallas_call | solution.py:58
  12.9 21.1 %all_to_all.5 = s16[32,2,3712]{2,1,0:T(2,128)(2,1)S(1)} all-to-all(s16[32,2,3712]{2,1,0:T(2,128)(2,1)} %shard_map.55), channel_id=1, replica_groups=mesh['group'=32,'local'=16] {'group'}, dimensions={0} | all-to-all | bytes 950272 | tf_op jit(solution)/shard_map/all_to_all | solution.py:175
  34.0 0.0 collective-permute-done
  34.0 0.0 collective-permute-done.1
  34.0 0.2 reshape.9
  34.2 0.0 copy-start
  34.2 0.0 copy-start.1
  34.2 39.7 %all-gather.1 = s16[8,64,3712]{2,1,0:T(8,128)(2,1)S(1)} all-gather(s16[1,64,3712]{2,1,0:T(8,128)(2,1)S(1)} %reshape.9), channel_id=1, replica_groups={{0,2,4,6,8,10,12,14},{1,3,5,7,9,11,13,15},{16,18,20,22,24,26,28,30},{17..., dimensions={0}, use_global_device_ids=true | all-gather | bytes 4276224 | tf_op jit(solution)/shard_map/all_gather | solution.py:180
  74.0 0.0 copy-done
  74.0 0.0 copy-done.1
  74.0 5.3 %shard_map.56 = (bf16[512,256]{1,0:T(8,128)(2,1)S(1)}, bf16[512,256]{1,0:T(8,128)(2,1)S(1)}) custom-call(s16[512,3712]{1,0:T(8,128)(2,1)S(1)} %bitcast.6, bf16[3584,256]{1,0:T(8,128)(2,1)S(1)} %bitcast.7, bf16[3584,256]{1,0:T(8,128)(2,1)S(1)} %bitcast.8, bf16[3584,256]{1,0:T(8,128)(2,1)S(1)} %bitcast.9, bf16[3584,256]{1,0:T(8,128)(2,1)} %bitcast.4.up_of_other_ref), custom_call_target="tpu_custom_call" | custom-call | flops 3760000000 | bytes 12000000 | tf_op jit(solution)/shard_map/pallas_call | solution.py:91
  79.3 6.1 %collective-permute-start.2 = (bf16[512,256]{1,0:T(8,128)(2,1)S(1)}, bf16[512,256]{1,0:T(8,128)(2,1)S(1)}, u32[]{:S(2)}, u32[]{:S(2)}) collective-permute-start(bf16[512,256]{1,0:T(8,128)(2,1)S(1)} %get-tuple-element.14), channel_id=1, source_target_pairs={{0,1},{1,0},{2,3},{3,2},{4,5},{5,4},{6,7},{7,6},{8,9},{9,8},{10,11... | collective-permute-start | bytes 786440 | tf_op jit(solution)/shard_map/ppermute | solution.py:184
  85.4 1.1 %collective-permute-done.2.other_ref = bf16[512,256]{1,0:T(8,128)(2,1)S(1)} collective-permute-done((bf16[512,256]{1,0:T(8,128)(2,1)S(1)}, bf16[512,256]{1,0:T(8,128)(2,1)S(1)}, u32[]{:S(2)}, u32[]{:S(2)}) %collective-permute-start.2) | collective-permute-done | bytes 262176 | tf_op jit(solution)/shard_map/ppermute | solution.py:184
  86.6 1.5 %shard_map.57 = bf16[1024,256]{1,0:T(8,128)(2,1)} custom-call(bf16[512,256]{1,0:T(8,128)(2,1)S(1)} %get-tuple-element.13.own_ref, bf16[512,256]{1,0:T(8,128)(2,1)S(1)} %collective-permute-done.2.other_ref), custom_call_target="tpu_custom_call" | custom-call | bytes 1000000 | tf_op jit(solution)/shard_map/pallas_call | solution.py:148
Async XLA Ops:
  0.0 34.0 %collective-permute-start = (bf16[1,3584,256]{2,1,0:T(8,128)(2,1)}, bf16[1,3584,256]{2,1,0:T(8,128)(2,1)S(1)}, u32[]{:S(2)}, u32[]{:S(2)}) collective-permute-start(bf16[1,3584,256]{2,1,0:T(8,128)(2,1)} %param.8), channel_id=1, source_target_pairs={{0,1},{1,0},{2,3},{3,2},{4,5},{5,4},{6,7},{7,6},{8,9},{9,8},{10,11... | collective-permute-start | bytes 5505032 | tf_op jit(solution)/shard_map/ppermute | solution.py:176
  8.7 25.3 %collective-permute-start.1 = (bf16[1,3584,256]{2,1,0:T(8,128)(2,1)}, bf16[1,3584,256]{2,1,0:T(8,128)(2,1)}, u32[]{:S(2)}, u32[]{:S(2)}) collective-permute-start(bf16[1,3584,256]{2,1,0:T(8,128)(2,1)} %param.9), channel_id=1, source_target_pairs={{0,1},{1,0},{2,3},{3,2},{4,5},{5,4},{6,7},{7,6},{8,9},{9,8},{10,11... | collective-permute-start | bytes 5505032 | tf_op jit(solution)/shard_map/ppermute | solution.py:177
  34.2 39.8 %copy-start = (bf16[1,3584,256]{2,1,0:T(8,128)(2,1)S(1)}, bf16[1,3584,256]{2,1,0:T(8,128)(2,1)}, u32[]{:S(2)}) copy-start(bf16[1,3584,256]{2,1,0:T(8,128)(2,1)} %param.8) | copy-start | bytes 5505028
  34.2 39.8 %copy-start.1 = (bf16[1,3584,256]{2,1,0:T(8,128)(2,1)S(1)}, bf16[1,3584,256]{2,1,0:T(8,128)(2,1)}, u32[]{:S(2)}) copy-start(bf16[1,3584,256]{2,1,0:T(8,128)(2,1)} %param.9) | copy-start | bytes 5505028
  79.3 7.2 %collective-permute-start.2 = (bf16[512,256]{1,0:T(8,128)(2,1)S(1)}, bf16[512,256]{1,0:T(8,128)(2,1)S(1)}, u32[]{:S(2)}, u32[]{:S(2)}) collective-permute-start(bf16[512,256]{1,0:T(8,128)(2,1)S(1)} %get-tuple-element.14), channel_id=1, source_target_pairs={{0,1},{1,0},{2,3},{3,2},{4,5},{5,4},{6,7},{7,6},{8,9},{9,8},{10,11... | collective-permute-start | bytes 786440 | tf_op jit(solution)/shard_map/ppermute | solution.py:184

commit v5 on v3

--- a/solution.py
+++ b/solution.py
@@ -16,7 +16,7 @@
 EXP_BIAS = 200.0
 
 
-def pack_kernel(tokens_ref, routes_ref, gates_ref, out_ref):
+def pack_kernel(tokens_ref, routes_ref, gates_ref, out_ref, staged, sent):
     count, width = tokens_ref.shape
     n_group, per_group, packed_width = out_ref.shape
     rows = n_group * per_group
@@ -40,6 +40,8 @@
     chosen = jnp.where(token // BLOCK == row % per_group, chosen, 0.0)
     chosen = chosen.T.astype(jnp.bfloat16)
 
+    copies = []
+
     def send(values, first, size):
         high = jnp.floor(values * (1.0 / 256.0))
         low = values - 256.0 * high
@@ -47,10 +49,18 @@
         picked += jnp.dot(chosen, low.astype(jnp.bfloat16), preferred_element_type=jnp.float32)
         picked = picked.astype(jnp.int32).astype(jnp.int16)
         for group in range(n_group):
-            out_ref[group, :, first : first + size] = picked[group * per_group : (group + 1) * per_group]
-
-    send(codes, 0, width)
+            staged[group, :, first : first + size] = picked[group * per_group : (group + 1) * per_group]
+        cols = pl.ds(first, size)
+        copy = pltpu.make_async_copy(staged.at[:, :, cols], out_ref.at[:, :, cols], sent.at[len(copies)])
+        copy.start()
+        copies.append(copy)
+
     send(side, width, experts)
+    piece = width // CHUNKS
+    for chunk in range(CHUNKS):
+        send(codes[:, chunk * piece : (chunk + 1) * piece], chunk * piece, piece)
+    for copy in copies:
+        copy.wait()
 
 
 def pack_rows(tokens, routes, route_gates, n_group, experts):
@@ -59,43 +69,73 @@
         pack_kernel,
         out_shape=jax.ShapeDtypeStruct((n_group, count // BLOCK, width + experts), jnp.int16),
         in_specs=[pl.BlockSpec(memory_space=pltpu.VMEM)] * 3,
-        out_specs=pl.BlockSpec(memory_space=pltpu.VMEM),
+        out_specs=pl.BlockSpec(memory_space=pl.ANY),
+        scratch_shapes=[
+            pltpu.VMEM((n_group, count // BLOCK, width + experts), jnp.int16),
+            pltpu.SemaphoreType.DMA((CHUNKS + 1,)),
+        ],
     )(tokens, routes, route_gates)
 
 
-def hidden_kernel(codes_ref, gate_ref, up_ref, out_ref, rows, held_up, arrived):
-    width = rows.shape[1]
-    copy = pltpu.make_async_copy(up_ref, held_up, arrived)
-    copy.start()
+def scale_and_weight(side_ref):
     expert = lax.axis_index("group") * EXP_MESH + lax.axis_index("local") // (lax.axis_size("local") // EXP_MESH)
-    rows[...] = codes_ref[:, :width].astype(jnp.float32).astype(jnp.bfloat16)
-    side = codes_ref[:, width:].astype(jnp.float32)
+    side = side_ref[...].astype(jnp.float32)
     lane = lax.broadcasted_iota(jnp.int32, side.shape, 1)
     weight = jnp.sum(jnp.where(lane == expert, jnp.maximum(side, 0.0), 0.0), axis=1, keepdims=True)
-    weight = weight * (1.0 / GATE_ONE)
-    scale = jnp.exp2(jnp.min(side, axis=1, keepdims=True) + EXP_BIAS)
-    pre_gate = jnp.dot(rows[...], gate_ref[...], preferred_element_type=jnp.float32) * scale
+    return jnp.exp2(jnp.min(side, axis=1, keepdims=True) + EXP_BIAS), weight * (1.0 / GATE_ONE)
+
+
+def gated(pre_gate, pre_up, scale, weight, out_ref):
+    pre_gate = pre_gate * scale
+    out_ref[...] = (pre_gate / (1.0 + jnp.exp(-pre_gate)) * (pre_up * scale) * weight).astype(out_ref.dtype)
+
+
+def other_kernel(codes_ref, gate_ref, up_hbm, gate_later, up_later, out_ref, rows, held, arrived):
+    width = rows.shape[1]
+    copy = pltpu.make_async_copy(up_hbm, held, arrived)
+    copy.start()
+    rows[...] = codes_ref[:, :width].astype(jnp.float32).astype(jnp.bfloat16)
+    scale, weight = scale_and_weight(codes_ref.at[:, width:])
+    pre_gate = jnp.dot(rows[...], gate_ref[...], preferred_element_type=jnp.float32)
     copy.wait()
-    pre_up = jnp.dot(rows[...], held_up[...], preferred_element_type=jnp.float32) * scale
-    out_ref[...] = (pre_gate / (1.0 + jnp.exp(-pre_gate)) * pre_up * weight).astype(out_ref.dtype)
-
-
-def hidden(codes, width, gate, up):
+    pre_up = jnp.dot(rows[...], held[...], preferred_element_type=jnp.float32)
+    gated(pre_gate, pre_up, scale, weight, out_ref)
+
+
+def own_kernel(codes_ref, rows, gate_ref, up_ref, out_ref):
+    scale, weight = scale_and_weight(codes_ref.at[:, rows.shape[1] :])
+    pre_gate = jnp.dot(rows[...], gate_ref[...], preferred_element_type=jnp.float32)
+    pre_up = jnp.dot(rows[...], up_ref[...], preferred_element_type=jnp.float32)
+    gated(pre_gate, pre_up, scale, weight, out_ref)
+
+
+def hidden_of_other(codes, width, gate, up, gate_later, up_later):
     count = codes.shape[0]
-    out_dim = gate.shape[1]
-    return pl.pallas_call(
-        hidden_kernel,
-        out_shape=jax.ShapeDtypeStruct((count, out_dim), jnp.bfloat16),
-        in_specs=[pl.BlockSpec(memory_space=pltpu.VMEM)] * 2 + [pl.BlockSpec(memory_space=pl.ANY)],
-        out_specs=pl.BlockSpec(memory_space=pltpu.VMEM),
-        scratch_shapes=[
-            pltpu.VMEM((count, width), jnp.bfloat16),
-            pltpu.VMEM(up.shape, up.dtype),
-            pltpu.SemaphoreType.DMA,
+    in_vmem = pl.BlockSpec(memory_space=pltpu.VMEM)
+    return pl.pallas_call(
+        other_kernel,
+        out_shape=[
+            jax.ShapeDtypeStruct((count, gate.shape[1]), jnp.bfloat16),
+            jax.ShapeDtypeStruct((count, width), jnp.bfloat16),
         ],
+        in_specs=[in_vmem, in_vmem, pl.BlockSpec(memory_space=pl.ANY), in_vmem, in_vmem],
+        out_specs=[in_vmem, in_vmem],
+        scratch_shapes=[pltpu.VMEM(up.shape, up.dtype), pltpu.SemaphoreType.DMA],
         compiler_params=pltpu.CompilerParams(vmem_limit_bytes=16 << 20),
-        cost_estimate=pl.CostEstimate(flops=1880000000, bytes_accessed=8000000, transcendentals=131072),
-    )(codes, gate, up)
+        cost_estimate=pl.CostEstimate(flops=1880000000, bytes_accessed=12000000, transcendentals=131072),
+    )(codes, gate, up, gate_later, up_later)
+
+
+def hidden_of_own(codes, rows, gate, up):
+    in_vmem = pl.BlockSpec(memory_space=pltpu.VMEM)
+    return pl.pallas_call(
+        own_kernel,
+        out_shape=jax.ShapeDtypeStruct((rows.shape[0], gate.shape[1]), jnp.bfloat16),
+        in_specs=[in_vmem] * 4,
+        out_specs=in_vmem,
+        compiler_params=pltpu.CompilerParams(vmem_limit_bytes=16 << 20),
+        cost_estimate=pl.CostEstimate(flops=1880000000, bytes_accessed=12000000, transcendentals=131072),
+    )(codes, rows, gate, up)
 
 
 def interleave_kernel(own_ref, other_ref, out_ref, staged, ordered, done, sent, *, n_y, per_group):
@@ -175,9 +215,11 @@
     gathered = lax.all_gather(received, "local", axis=0, axis_index_groups=same_core, tiled=True)
     gathered = gathered.reshape(-1, width + experts)
 
-    for_other = hidden(gathered, width, other_gate[0], other_up[0])
+    for_other, rows = hidden_of_other(
+        gathered, width, other_gate[0], other_up[0], gate_weight[0], up_weight[0]
+    )
     from_other = lax.ppermute(for_other, "local", swap)
-    own = hidden(gathered, width, gate_weight[0], up_weight[0])
+    own = hidden_of_own(gathered, rows, gate_weight[0], up_weight[0])
     out = interleave(own, from_other, n_y, per_group)
     return out.reshape((1,) + out.shape)
 

time: 91.6 us -> 88.1 us (0.962)
  Pallas kernels: 13.4 us -> 9.85 us
    pallas_call x2, Pallas kernels: 9.69 us -> 6.24 us  [the longest x1 4.1 us: hidden_of_other(): pl.pallas_call(other_kernel, out_shape=[jax.ShapeDtypeStruct((count, gate...]
  transfers between devices with their start and end apart: 3 -> 3, of which waited for: 0 -> 0; matrix products, arithmetic and copies ran while one was open for 0% -> 0% of each run, Pallas kernels for 7% -> 5%
where the time goes in v5:
time: 88.1 us; the launch traced here: 87.8 us
  blocking collectives  60.9 us (69%)
  starting transfers between devices  16.8 us (19%)
  Pallas kernels  9.85 us (11%)
    all_gather x1, blocking collectives, shards(): lax.all_gather(received, 'local', axis=0, axis_index_groups=same_core, ti...  39.7 us
    all_to_all x1, blocking collectives, shards(): lax.all_to_all(packed, 'group', split_axis=0, concat_axis=0, tiled=True)  21.1 us
    ppermute x1, starting transfers between devices, shards(): other_gate = lax.ppermute(gate_weight, 'local', swap)  8.74 us
    ppermute x1, starting transfers between devices, shards(): from_other = lax.ppermute(for_other, 'local', swap)  6.09 us
    pallas_call x1, Pallas kernels, hidden_of_other(): pl.pallas_call(other_kernel, out_shape=[jax.ShapeDtypeStruct((count, gate...  4.1 us
    pallas_call x1, Pallas kernels, hidden_of_own(): pl.pallas_call(own_kernel, out_shape=jax.ShapeDtypeStruct((rows.shape[0],...  2.14 us
    pallas_call x1, Pallas kernels, pack_rows(): pl.pallas_call(pack_kernel, out_shape=jax.ShapeDtypeStruct((n_group, coun...  2.1 us
    ppermute x1, starting transfers between devices, shards(): other_up = lax.ppermute(up_weight, 'local', swap)  1.92 us
  transfers between devices with their start and end apart: 3, of which 0 were waited for; matrix products, arithmetic and copies ran while one was open for 0% of the time, Pallas kernels for 5%

profile of v5, /device:TPU:1, one launch (start us, length us, event | category | flops | bytes accessed | tf_op | source)
XLA Modules:
  0.0 87.8 jit_solution(14470336402419408471)
XLA Ops:
  0.0 8.7 %collective-permute-start = (bf16[1,3584,256]{2,1,0:T(8,128)(2,1)}, bf16[1,3584,256]{2,1,0:T(8,128)(2,1)S(1)}, u32[]{:S(2)}, u32[]{:S(2)}) collective-permute-start(bf16[1,3584,256]{2,1,0:T(8,128)(2,1)} %param.8), channel_id=1, source_target_pairs={{0,1},{1,0},{2,3},{3,2},{4,5},{5,4},{6,7},{7,6},{8,9},{9,8},{10,11... | collective-permute-start | bytes 5505032 | tf_op jit(solution)/shard_map/ppermute | solution.py:211
  8.7 1.9 %collective-permute-start.1 = (bf16[1,3584,256]{2,1,0:T(8,128)(2,1)}, bf16[1,3584,256]{2,1,0:T(8,128)(2,1)}, u32[]{:S(2)}, u32[]{:S(2)}) collective-permute-start(bf16[1,3584,256]{2,1,0:T(8,128)(2,1)} %param.9), channel_id=1, source_target_pairs={{0,1},{1,0},{2,3},{3,2},{4,5},{5,4},{6,7},{7,6},{8,9},{9,8},{10,11... | collective-permute-start | bytes 5505032 | tf_op jit(solution)/shard_map/ppermute | solution.py:212
  10.7 2.1 %shard_map.55 = s16[32,2,3712]{2,1,0:T(2,128)(2,1)} custom-call(bf16[8,3584]{1,0:T(8,128)(2,1)} %tokens_ref.1, s32[8,8]{1,0:T(8,128)} %routes_ref.1, f32[8,8]{1,0:T(8,128)} %gates_ref.1), custom_call_target="tpu_custom_call" | custom-call | tf_op jit(solution)/shard_map/pallas_call | solution.py:68
  12.8 21.1 %all_to_all.5 = s16[32,2,3712]{2,1,0:T(2,128)(2,1)S(1)} all-to-all(s16[32,2,3712]{2,1,0:T(2,128)(2,1)} %shard_map.55), channel_id=1, replica_groups=mesh['group'=32,'local'=16] {'group'}, dimensions={0} | all-to-all | bytes 950272 | tf_op jit(solution)/shard_map/all_to_all | solution.py:210
  33.9 0.0 collective-permute-done
  33.9 0.0 collective-permute-done.1
  33.9 0.2 reshape.9
  34.1 0.0 copy-start
  34.1 0.0 copy-start.1
  34.1 39.7 %all-gather.1 = s16[8,64,3712]{2,1,0:T(8,128)(2,1)S(1)} all-gather(s16[1,64,3712]{2,1,0:T(8,128)(2,1)S(1)} %reshape.9), channel_id=1, replica_groups={{0,2,4,6,8,10,12,14},{1,3,5,7,9,11,13,15},{16,18,20,22,24,26,28,30},{17..., dimensions={0}, use_global_device_ids=true | all-gather | bytes 4276224 | tf_op jit(solution)/shard_map/all_gather | solution.py:215
  73.9 0.0 copy-done
  73.9 0.0 copy-done.1
  73.9 4.1 %shard_map.56 = (bf16[512,256]{1,0:T(8,128)(2,1)S(1)}, bf16[512,3584]{1,0:T(8,128)(2,1)S(1)}) custom-call(s16[512,3712]{1,0:T(8,128)(2,1)S(1)} %bitcast.6, bf16[3584,256]{1,0:T(8,128)(2,1)S(1)} %bitcast.12, bf16[3584,256]{1,0:T(8,128)(2,1)} %bitcast.2.up_hbm, bf16[3584,256]{1,0:T(8,128)(2,1)S(1)} %bitcast.8, bf16[3584,256]{1,0:T(8,128)(2,1)S(1)} %bitcast.10), custom_call_target="tpu_custom_call" | custom-call | flops 1880000000 | bytes 12000000 | tf_op jit(solution)/shard_map/pallas_call | solution.py:115
  78.0 6.1 %collective-permute-start.2 = (bf16[512,256]{1,0:T(8,128)(2,1)S(1)}, bf16[512,256]{1,0:T(8,128)(2,1)S(1)}, u32[]{:S(2)}, u32[]{:S(2)}) collective-permute-start(bf16[512,256]{1,0:T(8,128)(2,1)S(1)} %get-tuple-element.14), channel_id=1, source_target_pairs={{0,1},{1,0},{2,3},{3,2},{4,5},{5,4},{6,7},{7,6},{8,9},{9,8},{10,11... | collective-permute-start | bytes 786440 | tf_op jit(solution)/shard_map/ppermute | solution.py:221
  84.1 2.1 %shard_map.57.own_ref = bf16[512,256]{1,0:T(8,128)(2,1)S(1)} custom-call(s16[512,3712]{1,0:T(8,128)(2,1)S(1)} %bitcast.7, bf16[512,3584]{1,0:T(8,128)(2,1)S(1)} %get-tuple-element.13.rows, bf16[3584,256]{1,0:T(8,128)(2,1)S(1)} %bitcast.9, bf16[3584,256]{1,0:T(8,128)(2,1)S(1)} %bitcast.11), custom_call_target="tpu_custom_call" | custom-call | flops 1880000000 | bytes 12000000 | tf_op jit(solution)/shard_map/pallas_call | solution.py:131
  86.3 0.0 collective-permute-done.2.other_ref
  86.3 1.5 %shard_map.58 = bf16[1024,256]{1,0:T(8,128)(2,1)} custom-call(bf16[512,256]{1,0:T(8,128)(2,1)S(1)} %shard_map.57.own_ref, bf16[512,256]{1,0:T(8,128)(2,1)S(1)} %collective-permute-done.2.other_ref), custom_call_target="tpu_custom_call" | custom-call | bytes 1000000 | tf_op jit(solution)/shard_map/pallas_call | solution.py:183
Async XLA Ops:
  0.0 33.9 %collective-permute-start = (bf16[1,3584,256]{2,1,0:T(8,128)(2,1)}, bf16[1,3584,256]{2,1,0:T(8,128)(2,1)S(1)}, u32[]{:S(2)}, u32[]{:S(2)}) collective-permute-start(bf16[1,3584,256]{2,1,0:T(8,128)(2,1)} %param.8), channel_id=1, source_target_pairs={{0,1},{1,0},{2,3},{3,2},{4,5},{5,4},{6,7},{7,6},{8,9},{9,8},{10,11... | collective-permute-start | bytes 5505032 | tf_op jit(solution)/shard_map/ppermute | solution.py:211
  8.7 25.2 %collective-permute-start.1 = (bf16[1,3584,256]{2,1,0:T(8,128)(2,1)}, bf16[1,3584,256]{2,1,0:T(8,128)(2,1)}, u32[]{:S(2)}, u32[]{:S(2)}) collective-permute-start(bf16[1,3584,256]{2,1,0:T(8,128)(2,1)} %param.9), channel_id=1, source_target_pairs={{0,1},{1,0},{2,3},{3,2},{4,5},{5,4},{6,7},{7,6},{8,9},{9,8},{10,11... | collective-permute-start | bytes 5505032 | tf_op jit(solution)/shard_map/ppermute | solution.py:212
  34.1 39.8 %copy-start = (bf16[1,3584,256]{2,1,0:T(8,128)(2,1)S(1)}, bf16[1,3584,256]{2,1,0:T(8,128)(2,1)}, u32[]{:S(2)}) copy-start(bf16[1,3584,256]{2,1,0:T(8,128)(2,1)} %param.8) | copy-start | bytes 5505028
  34.1 39.8 %copy-start.1 = (bf16[1,3584,256]{2,1,0:T(8,128)(2,1)S(1)}, bf16[1,3584,256]{2,1,0:T(8,128)(2,1)}, u32[]{:S(2)}) copy-start(bf16[1,3584,256]{2,1,0:T(8,128)(2,1)} %param.9) | copy-start | bytes 5505028
  78.0 8.3 %collective-permute-start.2 = (bf16[512,256]{1,0:T(8,128)(2,1)S(1)}, bf16[512,256]{1,0:T(8,128)(2,1)S(1)}, u32[]{:S(2)}, u32[]{:S(2)}) collective-permute-start(bf16[512,256]{1,0:T(8,128)(2,1)S(1)} %get-tuple-element.14), channel_id=1, source_target_pairs={{0,1},{1,0},{2,3},{3,2},{4,5},{5,4},{6,7},{7,6},{8,9},{9,8},{10,11... | collective-permute-start | bytes 786440 | tf_op jit(solution)/shard_map/ppermute | solution.py:221

commit v6 on v5

v6 whole, which is shorter than its diff:
```python
import functools

import jax
import jax.numpy as jnp
from jax import lax
from jax.experimental import pallas as pl
from jax.experimental.pallas import tpu as pltpu
from jax.sharding import PartitionSpec as P

EXP_MESH = 4
BLOCK = 4
CHUNKS = 4
GATE_ONE = 16000.0
CODE_MAX = 32000.0
EXP_BIAS = 200.0


def pack_kernel(tokens_ref, routes_ref, gates_ref, out_ref, staged, sent):
    count, width = tokens_ref.shape
    n_group, per_group, packed_width = out_ref.shape
    rows = n_group * per_group
    experts = packed_width - width
    tok = tokens_ref[...].astype(jnp.float32)
    largest = jnp.maximum(jnp.max(jnp.abs(tok), axis=1, keepdims=True), 1e-25)
    power = jnp.floor(jnp.log2(CODE_MAX / largest))
    codes = jnp.round(tok * jnp.exp2(power))
    routes = routes_ref[...]
    gate_codes = jnp.round(gates_ref[...] * GATE_ONE)
    expert = lax.broadcasted_iota(jnp.int32, (count, experts), 1)
    row = lax.broadcasted_iota(jnp.int32, (count, rows), 1)
    token = lax.broadcasted_iota(jnp.int32, (count, rows), 0)
    side = jnp.zeros((count, experts), jnp.float32)
    chosen = jnp.zeros((count, rows), jnp.float32)
    for k in range(routes.shape[1]):
        route = routes[:, k : k + 1]
        side = side + jnp.where(expert == route, gate_codes[:, k : k + 1], 0.0)
        chosen = jnp.where(route // EXP_MESH == row // per_group, 1.0, chosen)
    side = jnp.where(side > 0.0, side, -(power + EXP_BIAS))
    chosen = jnp.where(token // BLOCK == row % per_group, chosen, 0.0)
    chosen = chosen.T.astype(jnp.bfloat16)

    copies = []

    def send(values, first, size):
        high = jnp.floor(values * (1.0 / 256.0))
        low = values - 256.0 * high
        picked = jnp.dot(chosen, (256.0 * high).astype(jnp.bfloat16), preferred_element_type=jnp.float32)
        picked += jnp.dot(chosen, low.astype(jnp.bfloat16), preferred_element_type=jnp.float32)
        picked = picked.astype(jnp.int32).astype(jnp.int16)
        for group in range(n_group):
            staged[group, :, first : first + size] = picked[group * per_group : (group + 1) * per_group]
        cols = pl.ds(first, size)
        copy = pltpu.make_async_copy(staged.at[:, :, cols], out_ref.at[:, :, cols], sent.at[len(copies)])
        copy.start()
        copies.append(copy)

    send(side, width, experts)
    piece = width // CHUNKS
    for chunk in range(CHUNKS):
        send(codes[:, chunk * piece : (chunk + 1) * piece], chunk * piece, piece)
    for copy in copies:
        copy.wait()


def pack_rows(tokens, routes, route_gates, n_group, experts):
    count, width = tokens.shape
    return pl.pallas_call(
        pack_kernel,
        out_shape=jax.ShapeDtypeStruct((n_group, count // BLOCK, width + experts), jnp.int16),
        in_specs=[pl.BlockSpec(memory_space=pltpu.VMEM)] * 3,
        out_specs=pl.BlockSpec(memory_space=pl.ANY),
        scratch_shapes=[
            pltpu.VMEM((n_group, count // BLOCK, width + experts), jnp.int16),
            pltpu.SemaphoreType.DMA((CHUNKS + 1,)),
        ],
    )(tokens, routes, route_gates)


def scale_and_weight(side_ref):
    expert = lax.axis_index("group") * EXP_MESH + lax.axis_index("local") // (lax.axis_size("local") // EXP_MESH)
    side = side_ref[...].astype(jnp.float32)
    lane = lax.broadcasted_iota(jnp.int32, side.shape, 1)
    weight = jnp.sum(jnp.where(lane == expert, jnp.maximum(side, 0.0), 0.0), axis=1, keepdims=True)
    return jnp.exp2(jnp.min(side, axis=1, keepdims=True) + EXP_BIAS), weight * (1.0 / GATE_ONE)


def gated(pre_gate, pre_up, scale, weight):
    pre_gate = pre_gate * scale
    return (pre_gate / (1.0 + jnp.exp(-pre_gate)) * (pre_up * scale) * weight).astype(jnp.bfloat16)


def placement(core, n_y, per_group, rows):
    in_block = rows // n_y
    per_source = 2 * n_y * per_group
    at = lax.broadcasted_iota(jnp.int32, (2 * rows, 1), 0)
    pair = at // per_group
    source = (at % per_source) // (2 * per_group) * in_block + at // per_source * per_group + at % per_group
    source = jnp.where(pair % 2 == core, source, -1)
    return (lax.broadcasted_iota(jnp.int32, (2 * rows, rows), 1) == source).astype(jnp.float32).astype(jnp.bfloat16)


def other_kernel(codes_ref, gate_of_own, gate_ref, up_hbm, up_later, out_ref, own_gate_ref, rows, held, arrived):
    width = rows.shape[1]
    copy = pltpu.make_async_copy(up_hbm, held, arrived)
    copy.start()
    rows[...] = codes_ref[:, :width].astype(jnp.float32).astype(jnp.bfloat16)
    scale, weight = scale_and_weight(codes_ref.at[:, width:])
    own_gate_ref[...] = jnp.dot(rows[...], gate_of_own[...], preferred_element_type=jnp.float32)
    pre_gate = jnp.dot(rows[...], gate_ref[...], preferred_element_type=jnp.float32)
    copy.wait()
    pre_up = jnp.dot(rows[...], held[...], preferred_element_type=jnp.float32)
    out_ref[...] = gated(pre_gate, pre_up, scale, weight)


def own_kernel(codes_ref, rows, gate_of_own, up_ref, placed_ref, place_ref, *, n_y, per_group):
    core = lax.axis_index("local") % 2
    scale, weight = scale_and_weight(codes_ref.at[:, rows.shape[1] :])
    pre_up = jnp.dot(rows[...], up_ref[...], preferred_element_type=jnp.float32)
    own = gated(gate_of_own[...], pre_up, scale, weight)
    place = placement(core, n_y, per_group, rows.shape[0])
    placed_ref[...] = jnp.dot(place, own, preferred_element_type=jnp.float32).astype(placed_ref.dtype)
    place_ref[...] = placement(1 - core, n_y, per_group, rows.shape[0])


def join_kernel(placed_ref, place_ref, other_ref, out_hbm, joined, sent):
    piece = joined.shape[0] // CHUNKS
    copies = []
    for chunk in range(CHUNKS):
        rows = slice(chunk * piece, (chunk + 1) * piece)
        other = jnp.dot(place_ref[rows], other_ref[...], preferred_element_type=jnp.float32)
        joined[rows] = (placed_ref[rows].astype(jnp.float32) + other).astype(joined.dtype)
        copy = pltpu.make_async_copy(joined.at[rows], out_hbm.at[rows], sent.at[chunk])
        copy.start()
        copies.append(copy)
    for copy in copies:
        copy.wait()


def hidden_of_other(codes, width, gate_of_own, gate, up, up_later):
    count = codes.shape[0]
    out_dim = gate.shape[1]
    in_vmem = pl.BlockSpec(memory_space=pltpu.VMEM)
    return pl.pallas_call(
        other_kernel,
        out_shape=[
            jax.ShapeDtypeStruct((count, out_dim), jnp.bfloat16),
            jax.ShapeDtypeStruct((count, out_dim), jnp.float32),
            jax.ShapeDtypeStruct((count, width), jnp.bfloat16),
        ],
        in_specs=[in_vmem, in_vmem, in_vmem, pl.BlockSpec(memory_space=pl.ANY), in_vmem],
        out_specs=[in_vmem] * 3,
        scratch_shapes=[pltpu.VMEM(up.shape, up.dtype), pltpu.SemaphoreType.DMA],
        compiler_params=pltpu.CompilerParams(vmem_limit_bytes=16 << 20),
        cost_estimate=pl.CostEstimate(flops=2820000000, bytes_accessed=12000000, transcendentals=131072),
    )(codes, gate_of_own, gate, up, up_later)


def hidden_of_own(codes, rows, gate_of_own, up, n_y, per_group):
    count = rows.shape[0]
    in_vmem = pl.BlockSpec(memory_space=pltpu.VMEM)
    return pl.pallas_call(
        functools.partial(own_kernel, n_y=n_y, per_group=per_group),
        out_shape=[
            jax.ShapeDtypeStruct((2 * count, up.shape[1]), jnp.bfloat16),
            jax.ShapeDtypeStruct((2 * count, count), jnp.bfloat16),
        ],
        in_specs=[in_vmem] * 4,
        out_specs=[in_vmem] * 2,
        compiler_params=pltpu.CompilerParams(vmem_limit_bytes=16 << 20),
        cost_estimate=pl.CostEstimate(flops=940000000, bytes_accessed=12000000, transcendentals=131072),
    )(codes, rows, gate_of_own, up)


def join(placed, place, other):
    in_vmem = pl.BlockSpec(memory_space=pltpu.VMEM)
    return pl.pallas_call(
        join_kernel,
        out_shape=jax.ShapeDtypeStruct(placed.shape, placed.dtype),
        in_specs=[in_vmem] * 3,
        out_specs=pl.BlockSpec(memory_space=pl.ANY),
        scratch_shapes=[pltpu.VMEM(placed.shape, placed.dtype), pltpu.SemaphoreType.DMA((CHUNKS,))],
        compiler_params=pltpu.CompilerParams(vmem_limit_bytes=8 << 20),
        cost_estimate=pl.CostEstimate(flops=270000000, bytes_accessed=2000000, transcendentals=0),
    )(placed, place, other)


def shards(tokens, routes, route_gates, gate_weight, up_weight):
    n_group = lax.axis_size("group")
    n_local = lax.axis_size("local")
    n_y = n_local // 2
    width = tokens.shape[1]
    experts = n_group * EXP_MESH
    per_group = tokens.shape[0] // BLOCK
    swap = [(2 * y + c, 2 * y + 1 - c) for y in range(n_y) for c in range(2)]
    same_core = [[2 * y + c for y in range(n_y)] for c in range(2)]

    packed = pack_rows(tokens, routes, route_gates, n_group, experts)
    received = lax.all_to_all(packed, "group", split_axis=0, concat_axis=0, tiled=True)
    other_gate = lax.ppermute(gate_weight, "local", swap)
    other_up = lax.ppermute(up_weight, "local", swap)
    received, other_gate, other_up = lax.optimization_barrier((received, other_gate, other_up))
    received = received.reshape(1, n_group * per_group, width + experts)
    gathered = lax.all_gather(received, "local", axis=0, axis_index_groups=same_core, tiled=True)
    gathered = gathered.reshape(-1, width + experts)

    for_other, gate_of_own, rows = hidden_of_other(
        gathered, width, gate_weight[0], other_gate[0], other_up[0], up_weight[0]
    )
    from_other = lax.ppermute(for_other, "local", swap)
    placed, place = hidden_of_own(gathered, rows, gate_of_own, up_weight[0], n_y, per_group)
    out = join(placed, place, from_other)
    return out.reshape((1,) + out.shape)


def solution(mesh):
    placed = (
        P(("group", "local"), None),
        P(("group", "local"), None),
        P(("group", "local"), None),
        P(("group", "local"), None, None),
        P(("group", "local"), None, None),
    )
    return jax.shard_map(
        shards,
        mesh=mesh,
        in_specs=placed,
        out_specs=P(("group", "local"), None, None),
        check_vma=False,
    )
```

time: 88.1 us -> 90.1 us (1.023)
  Pallas kernels: 9.85 us -> 11.8 us
    pallas_call x3, Pallas kernels: 7.75 us -> 9.73 us  [the longest x1 6.2 us: hidden_of_other(): pl.pallas_call(other_kernel, out_shape=[jax.ShapeDtypeStruct((count, out_...]
where the time goes in v6:
time: 90.1 us; the launch traced here: 89.8 us
  blocking collectives  60.9 us (68%)
  starting transfers between devices  16.8 us (19%)
  Pallas kernels  11.8 us (13%)
    all_gather x1, blocking collectives, shards(): lax.all_gather(received, 'local', axis=0, axis_index_groups=same_core, ti...  39.7 us
    all_to_all x1, blocking collectives, shards(): lax.all_to_all(packed, 'group', split_axis=0, concat_axis=0, tiled=True)  21.1 us
    ppermute x1, starting transfers between devices, shards(): other_gate = lax.ppermute(gate_weight, 'local', swap)  8.74 us
    pallas_call x1, Pallas kernels, hidden_of_other(): pl.pallas_call(other_kernel, out_shape=[jax.ShapeDtypeStruct((count, out_...  6.2 us
    ppermute x1, starting transfers between devices, shards(): from_other = lax.ppermute(for_other, 'local', swap)  6.09 us
    pallas_call x1, Pallas kernels, hidden_of_own(): pl.pallas_call(functools.partial(own_kernel, n_y=n_y, per_group=per_group...  2.35 us
    pallas_call x1, Pallas kernels, pack_rows(): pl.pallas_call(pack_kernel, out_shape=jax.ShapeDtypeStruct((n_group, coun...  2.1 us
    ppermute x1, starting transfers between devices, shards(): other_up = lax.ppermute(up_weight, 'local', swap)  1.92 us
  transfers between devices with their start and end apart: 3, of which 0 were waited for; matrix products, arithmetic and copies ran while one was open for 0% of the time, Pallas kernels for 5%

profile of v6, /device:TPU:1, one launch (start us, length us, event | category | flops | bytes accessed | tf_op | source)
XLA Modules:
  0.0 89.8 jit_solution(9430262889155857978)
XLA Ops:
  0.0 8.7 %collective-permute-start = (bf16[1,3584,256]{2,1,0:T(8,128)(2,1)}, bf16[1,3584,256]{2,1,0:T(8,128)(2,1)S(1)}, u32[]{:S(2)}, u32[]{:S(2)}) collective-permute-start(bf16[1,3584,256]{2,1,0:T(8,128)(2,1)} %param.8), channel_id=1, source_target_pairs={{0,1},{1,0},{2,3},{3,2},{4,5},{5,4},{6,7},{7,6},{8,9},{9,8},{10,11... | collective-permute-start | bytes 5505032 | tf_op jit(solution)/shard_map/ppermute | solution.py:199
  8.7 1.9 %collective-permute-start.1 = (bf16[1,3584,256]{2,1,0:T(8,128)(2,1)}, bf16[1,3584,256]{2,1,0:T(8,128)(2,1)}, u32[]{:S(2)}, u32[]{:S(2)}) collective-permute-start(bf16[1,3584,256]{2,1,0:T(8,128)(2,1)} %param.9), channel_id=1, source_target_pairs={{0,1},{1,0},{2,3},{3,2},{4,5},{5,4},{6,7},{7,6},{8,9},{9,8},{10,11... | collective-permute-start | bytes 5505032 | tf_op jit(solution)/shard_map/ppermute | solution.py:200
  10.7 2.1 %shard_map.55 = s16[32,2,3712]{2,1,0:T(2,128)(2,1)} custom-call(bf16[8,3584]{1,0:T(8,128)(2,1)} %tokens_ref.1, s32[8,8]{1,0:T(8,128)} %routes_ref.1, f32[8,8]{1,0:T(8,128)} %gates_ref.1), custom_call_target="tpu_custom_call" | custom-call | tf_op jit(solution)/shard_map/pallas_call | solution.py:67
  12.8 21.1 %all_to_all.5 = s16[32,2,3712]{2,1,0:T(2,128)(2,1)S(1)} all-to-all(s16[32,2,3712]{2,1,0:T(2,128)(2,1)} %shard_map.55), channel_id=1, replica_groups=mesh['group'=32,'local'=16] {'group'}, dimensions={0} | all-to-all | bytes 950272 | tf_op jit(solution)/shard_map/all_to_all | solution.py:198
  33.9 0.0 collective-permute-done
  33.9 0.0 collective-permute-done.1
  33.9 0.2 reshape.9
  34.1 0.0 copy-start
  34.1 0.0 copy-start.1
  34.1 39.7 %all-gather.1 = s16[8,64,3712]{2,1,0:T(8,128)(2,1)S(1)} all-gather(s16[1,64,3712]{2,1,0:T(8,128)(2,1)S(1)} %reshape.9), channel_id=1, replica_groups={{0,2,4,6,8,10,12,14},{1,3,5,7,9,11,13,15},{16,18,20,22,24,26,28,30},{17..., dimensions={0}, use_global_device_ids=true | all-gather | bytes 4276224 | tf_op jit(solution)/shard_map/all_gather | solution.py:203
  73.9 0.0 copy-done
  73.9 0.0 copy-done.1
  73.9 6.2 %shard_map.56 = (bf16[512,256]{1,0:T(8,128)(2,1)S(1)}, f32[512,256]{1,0:T(8,128)S(1)}, bf16[512,3584]{1,0:T(8,128)(2,1)S(1)}) custom-call(s16[512,3712]{1,0:T(8,128)(2,1)S(1)} %bitcast.6, bf16[3584,256]{1,0:T(8,128)(2,1)S(1)} %bitcast.10, bf16[3584,256]{1,0:T(8,128)(2,1)S(1)} %bitcast.11, bf16[3584,256]{1,0:T(8,128)(2,1)} %bitcast.3.up_hbm, ...), custom_call_target="tpu_custom_call" | custom-call | flops 2820000000 | bytes 12000000 | tf_op jit(solution)/shard_map/pallas_call | solution.py:143
  80.1 6.1 %collective-permute-start.2 = (bf16[512,256]{1,0:T(8,128)(2,1)S(1)}, bf16[512,256]{1,0:T(8,128)(2,1)S(1)}, u32[]{:S(2)}, u32[]{:S(2)}) collective-permute-start(bf16[512,256]{1,0:T(8,128)(2,1)S(1)} %get-tuple-element.20), channel_id=1, source_target_pairs={{0,1},{1,0},{2,3},{3,2},{4,5},{5,4},{6,7},{7,6},{8,9},{9,8},{10,11... | collective-permute-start | bytes 786440 | tf_op jit(solution)/shard_map/ppermute | solution.py:209
  86.2 2.4 %shard_map.57 = (bf16[1024,256]{1,0:T(8,128)(2,1)S(1)}, bf16[1024,512]{1,0:T(8,128)(2,1)S(1)}) custom-call(s16[512,3712]{1,0:T(8,128)(2,1)S(1)} %bitcast.7, bf16[512,3584]{1,0:T(8,128)(2,1)S(1)} %get-tuple-element.16.rows, f32[512,256]{1,0:T(8,128)S(1)} %get-tuple-element.17.gate_of_own, bf16[3584,256]{1,0:T(8,128)(2,1)S(1)} %bitcast.9), custom_call_target="tpu_custom_call" | custom-call | flops 940000000 | bytes 12000000 | tf_op jit(solution)/shard_map/pallas_call | solution.py:161
  88.6 0.0 collective-permute-done.2.other_ref
  88.6 1.2 %shard_map.58 = bf16[1024,256]{1,0:T(8,128)(2,1)} custom-call(bf16[1024,256]{1,0:T(8,128)(2,1)S(1)} %get-tuple-element.18.placed_ref, bf16[1024,512]{1,0:T(8,128)(2,1)S(1)} %get-tuple-element.19.place_ref, bf16[512,256]{1,0:T(8,128)(2,1)S(1)} %collective-permute-done.2.other_ref), custom_call_target="tpu_custom_call" | custom-call | flops 270000000 | bytes 2000000 | tf_op jit(solution)/shard_map/pallas_call | solution.py:176
Async XLA Ops:
  0.0 33.9 %collective-permute-start = (bf16[1,3584,256]{2,1,0:T(8,128)(2,1)}, bf16[1,3584,256]{2,1,0:T(8,128)(2,1)S(1)}, u32[]{:S(2)}, u32[]{:S(2)}) collective-permute-start(bf16[1,3584,256]{2,1,0:T(8,128)(2,1)} %param.8), channel_id=1, source_target_pairs={{0,1},{1,0},{2,3},{3,2},{4,5},{5,4},{6,7},{7,6},{8,9},{9,8},{10,11... | collective-permute-start | bytes 5505032 | tf_op jit(solution)/shard_map/ppermute | solution.py:199
  8.7 25.2 %collective-permute-start.1 = (bf16[1,3584,256]{2,1,0:T(8,128)(2,1)}, bf16[1,3584,256]{2,1,0:T(8,128)(2,1)}, u32[]{:S(2)}, u32[]{:S(2)}) collective-permute-start(bf16[1,3584,256]{2,1,0:T(8,128)(2,1)} %param.9), channel_id=1, source_target_pairs={{0,1},{1,0},{2,3},{3,2},{4,5},{5,4},{6,7},{7,6},{8,9},{9,8},{10,11... | collective-permute-start | bytes 5505032 | tf_op jit(solution)/shard_map/ppermute | solution.py:200
  34.1 39.8 %copy-start = (bf16[1,3584,256]{2,1,0:T(8,128)(2,1)S(1)}, bf16[1,3584,256]{2,1,0:T(8,128)(2,1)}, u32[]{:S(2)}) copy-start(bf16[1,3584,256]{2,1,0:T(8,128)(2,1)} %param.9) | copy-start | bytes 5505028
  34.1 39.8 %copy-start.1 = (bf16[1,3584,256]{2,1,0:T(8,128)(2,1)S(1)}, bf16[1,3584,256]{2,1,0:T(8,128)(2,1)}, u32[]{:S(2)}) copy-start(bf16[1,3584,256]{2,1,0:T(8,128)(2,1)} %param.8) | copy-start | bytes 5505028
  80.1 8.5 %collective-permute-start.2 = (bf16[512,256]{1,0:T(8,128)(2,1)S(1)}, bf16[512,256]{1,0:T(8,128)(2,1)S(1)}, u32[]{:S(2)}, u32[]{:S(2)}) collective-permute-start(bf16[512,256]{1,0:T(8,128)(2,1)S(1)} %get-tuple-element.20), channel_id=1, source_target_pairs={{0,1},{1,0},{2,3},{3,2},{4,5},{5,4},{6,7},{7,6},{8,9},{9,8},{10,11... | collective-permute-start | bytes 786440 | tf_op jit(solution)/shard_map/ppermute | solution.py:209

commit v7 on v5

--- a/solution.py
+++ b/solution.py
@@ -96,8 +96,8 @@
     copy.start()
     rows[...] = codes_ref[:, :width].astype(jnp.float32).astype(jnp.bfloat16)
     scale, weight = scale_and_weight(codes_ref.at[:, width:])
+    copy.wait()
     pre_gate = jnp.dot(rows[...], gate_ref[...], preferred_element_type=jnp.float32)
-    copy.wait()
     pre_up = jnp.dot(rows[...], held[...], preferred_element_type=jnp.float32)
     gated(pre_gate, pre_up, scale, weight, out_ref)
 
@@ -156,14 +156,13 @@
             @pl.when(my_core == core)
             def _():
                 for lane in range(tiles):
-                    for y in range(n_y):
+                    for group in range(chunk * groups, (chunk + 1) * groups):
                         for i in range(per_group):
-                            start = y * in_block + chunk * groups * per_group + i
-                            origin = pl.ds(start, groups, stride=per_group)
+                            origin = pl.ds(group * per_group + i, n_y, stride=in_block)
                             for source in range(2):
                                 place = core if source == 0 else 1 - core
-                                target = chunk * groups * per_source + (2 * y + place) * per_group + i
-                                ordered[lane, pl.ds(target, groups, stride=per_source), :] = staged[
+                                target = group * per_source + place * per_group + i
+                                ordered[lane, pl.ds(target, n_y, stride=2 * per_group), :] = staged[
                                     lane, source, origin, :
                                 ]
 

time: 88.1 us -> 87.7 us (level)
  no operation moved by 1% of the time
where the time goes in v7:
time: 87.7 us; the launch traced here: 87.3 us
  blocking collectives  60.9 us (69%)
  starting transfers between devices  16.8 us (19%)
  Pallas kernels  9.35 us (11%)
    all_gather x1, blocking collectives, shards(): lax.all_gather(received, 'local', axis=0, axis_index_groups=same_core, ti...  39.7 us
    all_to_all x1, blocking collectives, shards(): lax.all_to_all(packed, 'group', split_axis=0, concat_axis=0, tiled=True)  21.1 us
    ppermute x1, starting transfers between devices, shards(): other_gate = lax.ppermute(gate_weight, 'local', swap)  8.74 us
    ppermute x1, starting transfers between devices, shards(): from_other = lax.ppermute(for_other, 'local', swap)  6.09 us
    pallas_call x1, Pallas kernels, hidden_of_other(): pl.pallas_call(other_kernel, out_shape=[jax.ShapeDtypeStruct((count, gate...  3.65 us
    pallas_call x1, Pallas kernels, hidden_of_own(): pl.pallas_call(own_kernel, out_shape=jax.ShapeDtypeStruct((rows.shape[0],...  2.14 us
    pallas_call x1, Pallas kernels, pack_rows(): pl.pallas_call(pack_kernel, out_shape=jax.ShapeDtypeStruct((n_group, coun...  2.1 us
    ppermute x1, starting transfers between devices, shards(): other_up = lax.ppermute(up_weight, 'local', swap)  1.92 us
  transfers between devices with their start and end apart: 3, of which 0 were waited for; matrix products, arithmetic and copies ran while one was open for 0% of the time, Pallas kernels for 5%

profile of v7, /device:TPU:1, one launch (start us, length us, event | category | flops | bytes accessed | tf_op | source)
XLA Modules:
  0.0 87.3 jit_solution(10891807238931089452)
XLA Ops:
  0.0 8.7 %collective-permute-start = (bf16[1,3584,256]{2,1,0:T(8,128)(2,1)}, bf16[1,3584,256]{2,1,0:T(8,128)(2,1)S(1)}, u32[]{:S(2)}, u32[]{:S(2)}) collective-permute-start(bf16[1,3584,256]{2,1,0:T(8,128)(2,1)} %param.8), channel_id=1, source_target_pairs={{0,1},{1,0},{2,3},{3,2},{4,5},{5,4},{6,7},{7,6},{8,9},{9,8},{10,11... | collective-permute-start | bytes 5505032 | tf_op jit(solution)/shard_map/ppermute | solution.py:210
  8.7 1.9 %collective-permute-start.1 = (bf16[1,3584,256]{2,1,0:T(8,128)(2,1)}, bf16[1,3584,256]{2,1,0:T(8,128)(2,1)}, u32[]{:S(2)}, u32[]{:S(2)}) collective-permute-start(bf16[1,3584,256]{2,1,0:T(8,128)(2,1)} %param.9), channel_id=1, source_target_pairs={{0,1},{1,0},{2,3},{3,2},{4,5},{5,4},{6,7},{7,6},{8,9},{9,8},{10,11... | collective-permute-start | bytes 5505032 | tf_op jit(solution)/shard_map/ppermute | solution.py:211
  10.7 2.1 %shard_map.55 = s16[32,2,3712]{2,1,0:T(2,128)(2,1)} custom-call(bf16[8,3584]{1,0:T(8,128)(2,1)} %tokens_ref.1, s32[8,8]{1,0:T(8,128)} %routes_ref.1, f32[8,8]{1,0:T(8,128)} %gates_ref.1), custom_call_target="tpu_custom_call" | custom-call | tf_op jit(solution)/shard_map/pallas_call | solution.py:68
  12.8 21.1 %all_to_all.5 = s16[32,2,3712]{2,1,0:T(2,128)(2,1)S(1)} all-to-all(s16[32,2,3712]{2,1,0:T(2,128)(2,1)} %shard_map.55), channel_id=1, replica_groups=mesh['group'=32,'local'=16] {'group'}, dimensions={0} | all-to-all | bytes 950272 | tf_op jit(solution)/shard_map/all_to_all | solution.py:209
  33.9 0.0 collective-permute-done
  33.9 0.0 collective-permute-done.1
  33.9 0.2 reshape.9
  34.1 0.0 copy-start
  34.1 0.0 copy-start.1
  34.1 39.7 %all-gather.1 = s16[8,64,3712]{2,1,0:T(8,128)(2,1)S(1)} all-gather(s16[1,64,3712]{2,1,0:T(8,128)(2,1)S(1)} %reshape.9), channel_id=1, replica_groups={{0,2,4,6,8,10,12,14},{1,3,5,7,9,11,13,15},{16,18,20,22,24,26,28,30},{17..., dimensions={0}, use_global_device_ids=true | all-gather | bytes 4276224 | tf_op jit(solution)/shard_map/all_gather | solution.py:214
  73.9 0.0 copy-done
  73.9 0.0 copy-done.1
  73.9 3.6 %shard_map.56 = (bf16[512,256]{1,0:T(8,128)(2,1)S(1)}, bf16[512,3584]{1,0:T(8,128)(2,1)S(1)}) custom-call(s16[512,3712]{1,0:T(8,128)(2,1)S(1)} %bitcast.6, bf16[3584,256]{1,0:T(8,128)(2,1)S(1)} %bitcast.12, bf16[3584,256]{1,0:T(8,128)(2,1)} %bitcast.2.up_hbm, bf16[3584,256]{1,0:T(8,128)(2,1)S(1)} %bitcast.8, bf16[3584,256]{1,0:T(8,128)(2,1)S(1)} %bitcast.10), custom_call_target="tpu_custom_call" | custom-call | flops 1880000000 | bytes 12000000 | tf_op jit(solution)/shard_map/pallas_call | solution.py:115
  77.6 6.1 %collective-permute-start.2 = (bf16[512,256]{1,0:T(8,128)(2,1)S(1)}, bf16[512,256]{1,0:T(8,128)(2,1)S(1)}, u32[]{:S(2)}, u32[]{:S(2)}) collective-permute-start(bf16[512,256]{1,0:T(8,128)(2,1)S(1)} %get-tuple-element.14), channel_id=1, source_target_pairs={{0,1},{1,0},{2,3},{3,2},{4,5},{5,4},{6,7},{7,6},{8,9},{9,8},{10,11... | collective-permute-start | bytes 786440 | tf_op jit(solution)/shard_map/ppermute | solution.py:220
  83.7 2.1 %shard_map.57.own_ref = bf16[512,256]{1,0:T(8,128)(2,1)S(1)} custom-call(s16[512,3712]{1,0:T(8,128)(2,1)S(1)} %bitcast.7, bf16[512,3584]{1,0:T(8,128)(2,1)S(1)} %get-tuple-element.13.rows, bf16[3584,256]{1,0:T(8,128)(2,1)S(1)} %bitcast.9, bf16[3584,256]{1,0:T(8,128)(2,1)S(1)} %bitcast.11), custom_call_target="tpu_custom_call" | custom-call | flops 1880000000 | bytes 12000000 | tf_op jit(solution)/shard_map/pallas_call | solution.py:131
  85.8 0.0 collective-permute-done.2.other_ref
  85.8 1.5 %shard_map.58 = bf16[1024,256]{1,0:T(8,128)(2,1)} custom-call(bf16[512,256]{1,0:T(8,128)(2,1)S(1)} %shard_map.57.own_ref, bf16[512,256]{1,0:T(8,128)(2,1)S(1)} %collective-permute-done.2.other_ref), custom_call_target="tpu_custom_call" | custom-call | bytes 1000000 | tf_op jit(solution)/shard_map/pallas_call | solution.py:182
Async XLA Ops:
  0.0 33.9 %collective-permute-start = (bf16[1,3584,256]{2,1,0:T(8,128)(2,1)}, bf16[1,3584,256]{2,1,0:T(8,128)(2,1)S(1)}, u32[]{:S(2)}, u32[]{:S(2)}) collective-permute-start(bf16[1,3584,256]{2,1,0:T(8,128)(2,1)} %param.8), channel_id=1, source_target_pairs={{0,1},{1,0},{2,3},{3,2},{4,5},{5,4},{6,7},{7,6},{8,9},{9,8},{10,11... | collective-permute-start | bytes 5505032 | tf_op jit(solution)/shard_map/ppermute | solution.py:210
  8.7 25.2 %collective-permute-start.1 = (bf16[1,3584,256]{2,1,0:T(8,128)(2,1)}, bf16[1,3584,256]{2,1,0:T(8,128)(2,1)}, u32[]{:S(2)}, u32[]{:S(2)}) collective-permute-start(bf16[1,3584,256]{2,1,0:T(8,128)(2,1)} %param.9), channel_id=1, source_target_pairs={{0,1},{1,0},{2,3},{3,2},{4,5},{5,4},{6,7},{7,6},{8,9},{9,8},{10,11... | collective-permute-start | bytes 5505032 | tf_op jit(solution)/shard_map/ppermute | solution.py:211
  34.1 39.8 %copy-start = (bf16[1,3584,256]{2,1,0:T(8,128)(2,1)S(1)}, bf16[1,3584,256]{2,1,0:T(8,128)(2,1)}, u32[]{:S(2)}) copy-start(bf16[1,3584,256]{2,1,0:T(8,128)(2,1)} %param.8) | copy-start | bytes 5505028
  34.1 39.8 %copy-start.1 = (bf16[1,3584,256]{2,1,0:T(8,128)(2,1)S(1)}, bf16[1,3584,256]{2,1,0:T(8,128)(2,1)}, u32[]{:S(2)}) copy-start(bf16[1,3584,256]{2,1,0:T(8,128)(2,1)} %param.9) | copy-start | bytes 5505028
  77.6 8.3 %collective-permute-start.2 = (bf16[512,256]{1,0:T(8,128)(2,1)S(1)}, bf16[512,256]{1,0:T(8,128)(2,1)S(1)}, u32[]{:S(2)}, u32[]{:S(2)}) collective-permute-start(bf16[512,256]{1,0:T(8,128)(2,1)S(1)} %get-tuple-element.14), channel_id=1, source_target_pairs={{0,1},{1,0},{2,3},{3,2},{4,5},{5,4},{6,7},{7,6},{8,9},{9,8},{10,11... | collective-permute-start | bytes 786440 | tf_op jit(solution)/shard_map/ppermute | solution.py:220
